TPU v7x, 32 devices: a whole 2x2x4 slice. The times are simulated.
32 devices in a mesh: fsdp: 16 (over z, y, x), rep: 2 (over core).
Axes of the slice: x: 2, y: 2, z: 4, core: 2. Of those that a mesh axis runs over, the one named last changes fastest.
Arguments:
- tokens: bfloat16 [32, 1024, 768], P(('fsdp', 'rep')), may hold values from -6 to 6
- context: bfloat16 [32, 1024, 768], P(('fsdp', 'rep')), may hold values from -6 to 6
- clip_lengths: int32 [32], P(('fsdp', 'rep')), may hold values from 512 to 1024, as said below
- context_frames: int32 [32], P(('fsdp', 'rep')), may hold values from 1 to 4, as said below
- norm1_gain: bfloat16 [768], P('fsdp'), may hold values from 0.099609375 to 1.8984375
- norm1_bias: bfloat16 [768], P('fsdp'), may hold values from -1.5 to 1.5
- cross_q: bfloat16 [768, 768], P('fsdp'), may hold values from -0.21875 to 0.21875
- cross_k: bfloat16 [768, 768], P('fsdp'), may hold values from -0.21875 to 0.21875
- cross_v: bfloat16 [768, 768], P('fsdp'), may hold values from -0.21875 to 0.21875
- cross_out: bfloat16 [768, 768], P('fsdp'), may hold values from -4 to 4
- norm2_gain: bfloat16 [768], P('fsdp'), may hold values from 0.099609375 to 1.8984375
- norm2_bias: bfloat16 [768], P('fsdp'), may hold values from -1.5 to 1.5
- attn_qkv: bfloat16 [768, 2304], P('fsdp'), may hold values from -0.21875 to 0.21875
- attn_out: bfloat16 [768, 768], P('fsdp'), may hold values from -1.5 to 1.5
- norm3_gain: bfloat16 [768], P('fsdp'), may hold values from 0.099609375 to 1.8984375
- norm3_bias: bfloat16 [768], P('fsdp'), may hold values from -1.5 to 1.5
- mlp_up: bfloat16 [768, 3072], P('fsdp'), may hold values from -0.21875 to 0.21875
- mlp_down: bfloat16 [3072, 768], P('fsdp'), may hold values from -0.109375 to 0.109375
- cotangent: bfloat16 [32, 1024, 768], P(('fsdp', 'rep')), may hold values from -6 to 6
Outputs:
- block_out: bfloat16 [32, 1024, 768], P(('fsdp', 'rep'))
- input_grad: float32 [32, 1024, 768], P(('fsdp', 'rep'))
- grad_norm1_gain: float32 [768], P('fsdp')
- grad_norm1_bias: float32 [768], P('fsdp')
- grad_cross_q: float32 [768, 768], P('fsdp')
- grad_cross_k: float32 [768, 768], P('fsdp')
- grad_cross_v: float32 [768, 768], P('fsdp')
- grad_cross_out: float32 [768, 768], P('fsdp')
- grad_norm2_gain: float32 [768], P('fsdp')
- grad_norm2_bias: float32 [768], P('fsdp')
- grad_attn_qkv: float32 [768, 2304], P('fsdp')
- grad_attn_out: float32 [768, 768], P('fsdp')
- grad_norm3_gain: float32 [768], P('fsdp')
- grad_norm3_bias: float32 [768], P('fsdp')
- grad_mlp_up: float32 [768, 3072], P('fsdp')
- grad_mlp_down: float32 [3072, 768], P('fsdp')
Inputs may be any that keep to these rules, and one draw needn't show every extreme that they name: A clip's valid tokens fill its first clip_lengths slots; at least one clip has all 1024 slots valid. `context_frames`: A clip's valid context frames, of 256 tokens each, fill its first context slots; some clip has 4 valid frames and some clip has one.
All inputs are finite; a program needn't handle non-finite values.
Results may differ from a plain program's by a relative error of at most 0.019.
Values may be sent and summed in bfloat16 or wider, within the bound.
A program may use at most 384 MiB of HBM per device.

v0:
```python
import jax
import jax.numpy as jnp
from jax import lax
from jax.sharding import PartitionSpec as P

D = 768
HEAD = 64
HEADS = 12
FRAME_TOK = 256


epsilon = 1e-05


def cut_along(value, dim, count):
    shape = value.shape
    tiles = value.reshape(*shape[:dim], count, shape[dim] // count, *shape[dim + 1 :])
    return jnp.moveaxis(tiles, dim, 0)


def sum_at_owner(value, axis, dim):
    tiles = cut_along(value, dim, lax.axis_size(axis))
    arrived = lax.all_to_all(tiles, axis, split_axis=0, concat_axis=0, tiled=True)
    return arrived.astype(jnp.float32).sum(axis=0)


def side_by_side(arrays, axis, dim, along):
    columns = [a.reshape(*a.shape[:along], -1) for a in arrays]
    both = jnp.concatenate(columns, axis=along)
    filled, at, done = (sum_at_owner(both, axis, dim), 0, [])
    for a, column in zip(arrays, columns):
        piece = filled[..., at : at + column.shape[along]]
        done.append(piece.reshape(*piece.shape[:along], *a.shape[along:]))
        at += column.shape[along]
    return tuple(done)


def normalize(values, gain_row, bias_row):
    average = jnp.mean(values, -1, keepdims=True)
    centred = values - average
    variance = jnp.mean(centred * centred, -1, keepdims=True)
    return centred * lax.rsqrt(variance + epsilon) * gain_row + bias_row


def smooth_gate(values):
    return jax.nn.gelu(values, approximate=True)


def product(operand, matrix):
    return jnp.dot(operand, matrix, preferred_element_type=jnp.float32)


def against(operand, matrix):
    return lax.dot_general(
        operand, matrix, (((1,), (1,)), ((), ())), preferred_element_type=jnp.float32
    )


def transposed(operand, second):
    return lax.dot_general(
        operand, second, (((0,), (0,)), ((), ())), preferred_element_type=jnp.float32
    )


def split_heads(values):
    return values.reshape(values.shape[0], HEADS, values.shape[1] // HEADS)


def masked_scores(query_block, key_block, allowed, row_start, block_rows, key_span):
    scores = jnp.einsum(
        "qhd,khd->hqk", query_block, key_block, preferred_element_type=jnp.float32
    ) * HEAD ** (-0.5)
    return jnp.where(allowed(row_start, block_rows, key_span)[None], scores, -1e30)


def attend(queries, key_rows, value_rows, allowed, causal):
    row_count = queries.shape[0]
    block_rows = min(512, row_count)
    pieces = []
    log_sums = []
    for row_start in range(0, row_count, block_rows):
        key_span = row_start + block_rows if causal else key_rows.shape[0]
        query_block = split_heads(queries[row_start : row_start + block_rows])
        key_block = split_heads(key_rows[:key_span])
        value_block = split_heads(value_rows[:key_span])
        scores = masked_scores(query_block, key_block, allowed, row_start, block_rows, key_span)
        largest = jnp.max(scores, -1, keepdims=True)
        powers = jnp.exp(scores - largest)
        totals = jnp.sum(powers, -1, keepdims=True)
        weights = (powers / totals).astype(jnp.bfloat16)
        blended = jnp.einsum(
            "hqk,khd->qhd", weights, value_block, preferred_element_type=jnp.float32
        )
        pieces.append(blended.reshape(block_rows, -1))
        log_sums.append(largest + jnp.log(totals))
    return (jnp.concatenate(pieces, 0).astype(jnp.bfloat16), log_sums)


def attend_back(queries, key_rows, value_rows, grad_output, log_sums, allowed, causal):
    row_count = queries.shape[0]
    block_rows = min(512, row_count)
    query_parts = []
    grad_keys = jnp.zeros(key_rows.shape, jnp.float32)
    grad_values = jnp.zeros(value_rows.shape, jnp.float32)
    for position, row_start in enumerate(range(0, row_count, block_rows)):
        key_span = row_start + block_rows if causal else key_rows.shape[0]
        query_block = split_heads(queries[row_start : row_start + block_rows])
        key_block = split_heads(key_rows[:key_span])
        value_block = split_heads(value_rows[:key_span])
        grad_block = split_heads(grad_output[row_start : row_start + block_rows])
        scores = masked_scores(query_block, key_block, allowed, row_start, block_rows, key_span)
        chances = jnp.exp(scores - log_sums[position])
        grad_probs = jnp.einsum(
            "qhd,khd->hqk", grad_block, value_block, preferred_element_type=jnp.float32
        )
        inner_sum = jnp.sum(chances * grad_probs, -1, keepdims=True)
        grad_scores = (chances * (grad_probs - inner_sum)).astype(jnp.bfloat16)
        query_grad = jnp.einsum(
            "hqk,khd->qhd", grad_scores, key_block, preferred_element_type=jnp.float32
        ) * HEAD ** (-0.5)
        query_parts.append(query_grad.reshape(block_rows, -1))
        key_grad = jnp.einsum(
            "hqk,qhd->khd", grad_scores, query_block, preferred_element_type=jnp.float32
        ) * HEAD ** (-0.5)
        grad_keys = grad_keys.at[:key_span].add(key_grad.reshape(key_span, -1))
        value_grad = jnp.einsum(
            "hqk,qhd->khd",
            chances.astype(jnp.bfloat16),
            grad_block,
            preferred_element_type=jnp.float32,
        )
        grad_values = grad_values.at[:key_span].add(value_grad.reshape(key_span, -1))
    return (jnp.concatenate(query_parts, 0), grad_keys, grad_values)


def cross_forward(stream_in, context_rows, weight_set, allowed):
    gain_one, bias_one, cross_query, cross_key, cross_value, cross_proj = weight_set
    normed_f32, pull_one = jax.vjp(
        normalize, stream_in, gain_one.astype(jnp.float32), bias_one.astype(jnp.float32)
    )
    normed_one = normed_f32.astype(jnp.bfloat16)
    queries_one = product(normed_one, cross_query).astype(jnp.bfloat16)
    keys_one = product(context_rows, cross_key).astype(jnp.bfloat16)
    values_one = product(context_rows, cross_value).astype(jnp.bfloat16)
    attended_one, sums_one = attend(queries_one, keys_one, values_one, allowed, False)
    stream_mid = stream_in + product(attended_one, cross_proj)
    return (
        normed_one,
        queries_one,
        keys_one,
        values_one,
        attended_one,
        sums_one,
        stream_mid,
        pull_one,
    )


def block_forward(stream_mid, weight_set, allowed):
    gain_two, bias_two, joint_qkv, self_proj, gain_three, bias_three, expand, shrink = weight_set
    normed_f32, pull_two = jax.vjp(
        normalize, stream_mid, gain_two.astype(jnp.float32), bias_two.astype(jnp.float32)
    )
    normed_two = normed_f32.astype(jnp.bfloat16)
    joint_rows = product(normed_two, joint_qkv).astype(jnp.bfloat16)
    queries_two = joint_rows[:, :D]
    keys_two = joint_rows[:, D : 2 * D]
    values_two = joint_rows[:, 2 * D :]
    attended_two, sums_two = attend(queries_two, keys_two, values_two, allowed, True)
    stream_late = stream_mid + product(attended_two, self_proj)
    late_f32, pull_three = jax.vjp(
        normalize, stream_late, gain_three.astype(jnp.float32), bias_three.astype(jnp.float32)
    )
    normed_three = late_f32.astype(jnp.bfloat16)
    upward = product(normed_three, expand)
    activated, gelu_pull = jax.vjp(smooth_gate, upward)
    hidden = activated.astype(jnp.bfloat16)
    stream_out = stream_late + product(hidden, shrink)
    return (
        normed_two,
        queries_two,
        keys_two,
        values_two,
        attended_two,
        sums_two,
        pull_two,
        normed_three,
        pull_three,
        hidden,
        gelu_pull,
        stream_out,
    )


def shards(
    tokens,
    context,
    clip_lengths,
    context_frames,
    norm1_gain,
    norm1_bias,
    cross_q,
    cross_k,
    cross_v,
    cross_out,
    norm2_gain,
    norm2_bias,
    attn_qkv,
    attn_out,
    norm3_gain,
    norm3_bias,
    mlp_up,
    mlp_down,
    cotangent,
):
    stream_in = tokens[0].astype(jnp.float32)
    context_rows = context[0]
    valid_len = clip_lengths[0]
    frame_count = context_frames[0]
    slot_rows = stream_in.shape[0]

    def cross_allowed(row_start, block_rows, key_span):
        return jnp.broadcast_to(
            (jnp.arange(key_span) < frame_count * FRAME_TOK)[None, :], (block_rows, key_span)
        )

    def causal_allowed(row_start, block_rows, key_span):
        rows_here = row_start + jnp.arange(block_rows)[:, None]
        columns = jnp.arange(key_span)[None, :]
        return (columns <= rows_here) & (columns < valid_len)

    cross_full = (
        lax.all_gather(norm1_gain, "fsdp", axis=0, tiled=True),
        lax.all_gather(norm1_bias, "fsdp", axis=0, tiled=True),
        lax.all_gather(cross_q, "fsdp", axis=0, tiled=True),
        lax.all_gather(cross_k, "fsdp", axis=0, tiled=True),
        lax.all_gather(cross_v, "fsdp", axis=0, tiled=True),
        lax.all_gather(cross_out, "fsdp", axis=0, tiled=True),
    )
    stream_mid = cross_forward(stream_in, context_rows, cross_full, cross_allowed)[6]
    block_full = (
        lax.all_gather(norm2_gain, "fsdp", axis=0, tiled=True),
        lax.all_gather(norm2_bias, "fsdp", axis=0, tiled=True),
        lax.all_gather(attn_qkv, "fsdp", axis=0, tiled=True),
        lax.all_gather(attn_out, "fsdp", axis=0, tiled=True),
        lax.all_gather(norm3_gain, "fsdp", axis=0, tiled=True),
        lax.all_gather(norm3_bias, "fsdp", axis=0, tiled=True),
        lax.all_gather(mlp_up, "fsdp", axis=0, tiled=True),
        lax.all_gather(mlp_down, "fsdp", axis=0, tiled=True),
    )
    stream_top = block_forward(stream_mid, block_full, causal_allowed)[11]
    padding = (jnp.arange(slot_rows) < valid_len)[:, None]
    block_out = jnp.where(padding, stream_top, 0.0).astype(jnp.bfloat16)
    block_back = (
        lax.all_gather(norm2_gain, "fsdp", axis=0, tiled=True),
        lax.all_gather(norm2_bias, "fsdp", axis=0, tiled=True),
        lax.all_gather(attn_qkv, "fsdp", axis=0, tiled=True),
        lax.all_gather(attn_out, "fsdp", axis=0, tiled=True),
        lax.all_gather(norm3_gain, "fsdp", axis=0, tiled=True),
        lax.all_gather(norm3_bias, "fsdp", axis=0, tiled=True),
        lax.all_gather(mlp_up, "fsdp", axis=0, tiled=True),
        lax.all_gather(mlp_down, "fsdp", axis=0, tiled=True),
    )
    (
        normed_two,
        queries_two,
        keys_two,
        values_two,
        attended_two,
        sums_two,
        pull_two,
        normed_three,
        pull_three,
        hidden,
        gelu_pull,
        stream_unused,
    ) = block_forward(stream_mid, block_back, causal_allowed)
    grad_top = jnp.where(padding, cotangent[0].astype(jnp.float32), 0.0)
    grad_branch = grad_top.astype(jnp.bfloat16)
    grad_shrink = transposed(hidden, grad_branch)
    grad_upward = gelu_pull(against(grad_branch, block_back[7]))[0].astype(jnp.bfloat16)
    grad_expand = transposed(normed_three, grad_upward)
    grad_late, grad_gain_three, grad_bias_three = pull_three(against(grad_upward, block_back[6]))
    grad_late = grad_top + grad_late
    grad_attn = grad_late.astype(jnp.bfloat16)
    grad_self_proj = transposed(attended_two, grad_attn)
    grad_mixed = against(grad_attn, block_back[3]).astype(jnp.bfloat16)
    grad_query_two, grad_key_two, grad_value_two = attend_back(
        queries_two, keys_two, values_two, grad_mixed, sums_two, causal_allowed, True
    )
    grad_joint = jnp.concatenate([grad_query_two, grad_key_two, grad_value_two], 1).astype(
        jnp.bfloat16
    )
    grad_joint_qkv = transposed(normed_two, grad_joint)
    grad_mid, grad_gain_two, grad_bias_two = pull_two(against(grad_joint, block_back[2]))
    grad_mid = grad_late + grad_mid
    grad_scale = (slot_rows * tokens.shape[0] * lax.axis_size("fsdp") * lax.axis_size("rep")) ** (
        -0.5
    )
    block_terms = [
        grad * grad_scale
        for grad in (
            grad_gain_two,
            grad_bias_two,
            grad_joint_qkv,
            grad_self_proj,
            grad_gain_three,
            grad_bias_three,
            grad_expand,
            grad_shrink,
        )
    ]
    block_grads = (
        lax.psum_scatter(block_terms[0], "fsdp", scatter_dimension=0, tiled=True),
        lax.psum_scatter(block_terms[1], "fsdp", scatter_dimension=0, tiled=True),
        lax.psum_scatter(block_terms[2], "fsdp", scatter_dimension=0, tiled=True),
        lax.psum_scatter(block_terms[3], "fsdp", scatter_dimension=0, tiled=True),
        lax.psum_scatter(block_terms[4], "fsdp", scatter_dimension=0, tiled=True),
        lax.psum_scatter(block_terms[5], "fsdp", scatter_dimension=0, tiled=True),
        lax.psum_scatter(block_terms[6], "fsdp", scatter_dimension=0, tiled=True),
        lax.psum_scatter(block_terms[7], "fsdp", scatter_dimension=0, tiled=True),
    )
    cross_back = (
        lax.all_gather(norm1_gain, "fsdp", axis=0, tiled=True),
        lax.all_gather(norm1_bias, "fsdp", axis=0, tiled=True),
        lax.all_gather(cross_q, "fsdp", axis=0, tiled=True),
        lax.all_gather(cross_k, "fsdp", axis=0, tiled=True),
        lax.all_gather(cross_v, "fsdp", axis=0, tiled=True),
        lax.all_gather(cross_out, "fsdp", axis=0, tiled=True),
    )
    normed_one, queries_one, keys_one, values_one, attended_one, sums_one, mid_unused, pull_one = (
        cross_forward(stream_in, context_rows, cross_back, cross_allowed)
    )
    grad_cross = grad_mid.astype(jnp.bfloat16)
    grad_cross_proj = transposed(attended_one, grad_cross)
    grad_heard = against(grad_cross, cross_back[5]).astype(jnp.bfloat16)
    grad_query_one, grad_key_one, grad_value_one = attend_back(
        queries_one, keys_one, values_one, grad_heard, sums_one, cross_allowed, False
    )
    grad_query_one = grad_query_one.astype(jnp.bfloat16)
    grad_key_one = grad_key_one.astype(jnp.bfloat16)
    grad_value_one = grad_value_one.astype(jnp.bfloat16)
    grad_cross_query = transposed(normed_one, grad_query_one)
    grad_cross_key = transposed(context_rows, grad_key_one)
    grad_cross_value = transposed(context_rows, grad_value_one)
    grad_entry, grad_gain_one, grad_bias_one = pull_one(against(grad_query_one, cross_back[2]))
    input_grad = grad_mid + grad_entry
    cross_terms = [
        grad * grad_scale
        for grad in (
            grad_gain_one,
            grad_bias_one,
            grad_cross_query,
            grad_cross_key,
            grad_cross_value,
            grad_cross_proj,
        )
    ]
    cross_grads = (
        sum_at_owner(cross_terms[0].astype(jnp.bfloat16), "fsdp", 0),
        *side_by_side(
            (
                cross_terms[1].astype(jnp.bfloat16),
                cross_terms[2].astype(jnp.bfloat16),
                cross_terms[3].astype(jnp.bfloat16),
                cross_terms[4].astype(jnp.bfloat16),
                cross_terms[5].astype(jnp.bfloat16),
            ),
            "fsdp",
            0,
            1,
        ),
    )
    finals = (
        lax.psum(cross_grads[0].astype(jnp.bfloat16), "rep").astype(jnp.float32),
        lax.psum(cross_grads[1].astype(jnp.bfloat16), "rep").astype(jnp.float32),
        lax.psum(cross_grads[2].astype(jnp.bfloat16), "rep").astype(jnp.float32),
        lax.psum(cross_grads[3].astype(jnp.bfloat16), "rep").astype(jnp.float32),
        lax.psum(cross_grads[4].astype(jnp.bfloat16), "rep").astype(jnp.float32),
        lax.psum(cross_grads[5].astype(jnp.bfloat16), "rep").astype(jnp.float32),
        lax.psum(block_grads[0].astype(jnp.bfloat16), "rep").astype(jnp.float32),
        lax.psum(block_grads[1].astype(jnp.bfloat16), "rep").astype(jnp.float32),
        lax.psum(block_grads[2].astype(jnp.bfloat16), "rep").astype(jnp.float32),
        lax.psum(block_grads[3].astype(jnp.bfloat16), "rep").astype(jnp.float32),
        lax.psum(block_grads[4].astype(jnp.bfloat16), "rep").astype(jnp.float32),
        lax.psum(block_grads[5].astype(jnp.bfloat16), "rep").astype(jnp.float32),
        lax.psum(block_grads[6].astype(jnp.bfloat16), "rep").astype(jnp.float32),
        lax.psum(block_grads[7].astype(jnp.bfloat16), "rep").astype(jnp.float32),
    )
    return (
        block_out[None],
        input_grad[None],
        finals[0],
        finals[1],
        finals[2],
        finals[3],
        finals[4],
        finals[5],
        finals[6],
        finals[7],
        finals[8],
        finals[9],
        finals[10],
        finals[11],
        finals[12],
        finals[13],
    )


def solution(mesh):
    in_specs = (
        P(("fsdp", "rep"), None, None),
        P(("fsdp", "rep"), None, None),
        P(("fsdp", "rep")),
        P(("fsdp", "rep")),
        P("fsdp"),
        P("fsdp"),
        P("fsdp", None),
        P("fsdp", None),
        P("fsdp", None),
        P("fsdp", None),
        P("fsdp"),
        P("fsdp"),
        P("fsdp", None),
        P("fsdp", None),
        P("fsdp"),
        P("fsdp"),
        P("fsdp", None),
        P("fsdp", None),
        P(("fsdp", "rep"), None, None),
    )
    out_specs = (
        P(("fsdp", "rep"), None, None),
        P(("fsdp", "rep"), None, None),
        P("fsdp"),
        P("fsdp"),
        P("fsdp", None),
        P("fsdp", None),
        P("fsdp", None),
        P("fsdp", None),
        P("fsdp"),
        P("fsdp"),
        P("fsdp", None),
        P("fsdp", None),
        P("fsdp"),
        P("fsdp"),
        P("fsdp", None),
        P("fsdp", None),
    )
    return jax.shard_map(shards, mesh=mesh, in_specs=in_specs, out_specs=out_specs, check_vma=False)
```

profile of v0, /device:TPU:0, one launch (start us, length us, event | category | flops | bytes accessed | tf_op | source)
XLA Modules:
  0.0 1480.1 jit_solution(14409504446673390239)
XLA Ops:
  21.1 78.9 %all-reduce.13 = (bf16[768]{0:T(1024)(128)(2,1)S(1)}, bf16[768]{0:T(1024)(128)(2,1)S(1)}, bf16[768]{0:T(1024)(128)(2,1)S(1)}, bf16[768]{0:T(1024)(128)(2,1)S(1)}...) all-reduce(bf16[768]{0:T(1024)(128)(2,1)S(1)} %dynamic-update-slice, ...), channel_id=1, replica_groups=mesh['fsdp'=16,'rep'=2] {'fsdp'}, use_global_device_ids=true, to_apply=%add.3 | all-reduce | flops 4608 | bytes 18432
  111.9 15.6 %all-gather.13.cloned.1.call-done = bf16[768,768]{1,0:T(8,128)(2,1)} async-done(((bf16[48,768]{1,0:T(8,128)(2,1)}), bf16[768,768]{1,0:T(8,128)(2,1)}) %all-gather.13.cloned.1.call-update) | async-done | bytes 1179664 | tf_op jit(solution)/shard_map/all_gather | solution.py:236
  140.7 16.7 %fusion.26 = (f32[12,512]{1,0:T(8,128)S(1)}, f32[12,512]{1,0:T(8,128)S(1)}, f32[12,512,1024]{2,1,0:T(8,128)}) fusion(pred[1024]{0:T(1024)(128)(4,1)S(1)} %iota_compare_fusion.2, f32[12,512,1024]{2,1,0:T(8,128)} %fusion.125, bf16[512,12,64]{0,2,1:T(8,128)(2,1)} %bitcast.218, bf16[1024,12,64]{0,2,1:T(8,128)(2,1)} %bitcast.203), kind=kOutput, calls=%fused_computation.50 | convolution fusion | flops 843042816 | bytes 52741120 | tf_op jit(solution)/shard_map/qhd,khd->hqk/dot_general | solution.py:70
  157.4 18.9 %fusion = (f32[12,512]{1,0:T(8,128)S(1)}, f32[12,512]{1,0:T(8,128)S(1)}) fusion(f32[12,512]{1,0:T(8,128)S(1)} %get-tuple-element.218, f32[12,512,1024]{2,1,0:T(8,128)} %get-tuple-element.266, pred[1024]{0:T(1024)(128)(4,1)S(1)} %iota_compare_fusion.2, f32[12,512]{1,0:T(8,128)S(1)} %get-tuple-element.219, f32[12,512,1024]{2,1,0:T(8,128)} %fusion.125), kind=kLoop, calls=%fused_computation.18 | loop fusion | flops 50319360 | bytes 50430976 | tf_op jit(solution)/shard_map/reduce_sum | solution.py:89
  188.2 12.6 fusion.70
  200.8 12.4 fusion.69
  213.2 29.9 %all-gather.15.cloned.1.call-done = bf16[768,768]{1,0:T(8,128)(2,1)} async-done(((bf16[48,768]{1,0:T(8,128)(2,1)}), bf16[768,768]{1,0:T(8,128)(2,1)}) %all-gather.15.cloned.1.call-update) | async-done | bytes 1179664 | tf_op jit(solution)/shard_map/all_gather | solution.py:238
  248.5 67.4 %all-gather.17.cloned.1.call-done = bf16[768,2304]{1,0:T(8,128)(2,1)} async-done(((bf16[48,2304]{1,0:T(8,128)(2,1)}), bf16[768,2304]{1,0:T(8,128)(2,1)}) %all-gather.17.cloned.1.call-update) | async-done | bytes 3538960 | tf_op jit(solution)/shard_map/all_gather | solution.py:244
  365.5 12.3 fusion.2
  397.6 57.9 %all-gather.21.cloned.1.call-done = bf16[768,3072]{1,0:T(8,128)(2,1)} async-done(((bf16[48,3072]{1,0:T(8,128)(2,1)}), bf16[768,3072]{1,0:T(8,128)(2,1)}) %all-gather.21.cloned.1.call-update) | async-done | bytes 4718608 | tf_op jit(solution)/shard_map/all_gather | solution.py:248
  466.5 70.8 %all-gather.23.cloned.1.call-done = bf16[3072,768]{1,0:T(8,128)(2,1)} async-done(((bf16[192,768]{1,0:T(8,128)(2,1)}), bf16[3072,768]{1,0:T(8,128)(2,1)}) %all-gather.23.cloned.1.call-update) | async-done | bytes 4718608 | tf_op jit(solution)/shard_map/all_gather | solution.py:249
  537.4 14.7 fusion.12
  592.8 13.1 fusion.17
  605.9 18.4 %multiply_reduce_fusion.2 = (f32[12,512]{1,0:T(8,128)S(1)}, f32[12,512,1024]{2,1,0:T(8,128)}) fusion(f32[12,512]{1,0:T(8,128)S(1)} %log_add_fusion.2, f32[12,512,1024]{2,1,0:T(8,128)} %get-tuple-element.270, pred[512,1024]{1,0:T(8,128)(4,1)} %fusion.52, bf16[512,12,64]{0,2,1:T(8,128)(2,1)} %bitcast.237, bf16[1024,12,64]{0,2,1:T(8,128)(2,1)} %bitcast.225), kind=kOutput, calls=%fused_computation.7 | convolution fusion | flops 836757504 | bytes 53264384 | tf_op jit(solution)/shard_map/qhd,khd->hqk/dot_general | solution.py:113
  628.3 18.9 %multiply_convert_fusion.2 = bf16[12,512,1024]{2,1,0:T(8,128)(2,1)S(1)} fusion(f32[12,512,1024]{2,1,0:T(8,128)} %get-tuple-element.276, f32[12,512]{1,0:T(8,128)S(1)} %get-tuple-element.275, f32[12,512]{1,0:T(8,128)S(1)} %log_add_fusion.2, f32[12,512,1024]{2,1,0:T(8,128)} %get-tuple-element.270, pred[512,1024]{1,0:T(8,128)(4,1)} %fusion.52), kind=kLoop, calls=%fused_computation.6 | loop fusion | flops 37748736 | bytes 63488000 | tf_op jit(solution)/shard_map/convert_element_type | solution.py:117
  648.2 13.3 multiply_convert_fusion.3
  689.7 13.8 convolution_multiply_fusion.1
  759.2 12.9 add_convert_fusion
  772.2 36.8 %multiply_reduce_fusion.1 = (f32[12,512]{1,0:T(8,128)S(1)}, f32[12,512]{1,0:T(8,128)S(1)}, f32[12,512,1024]{2,1,0:T(8,128)}) fusion(f32[12,512]{1,0:T(8,128)S(1)} %get-tuple-element.287, f32[12,512,1024]{2,1,0:T(8,128)} %get-tuple-element.266, pred[1024]{0:T(1024)(128)(4,1)S(1)} %copy-done.87, f32[12,512,1024]{2,1,0:T(8,128)} %fusion.126, ...), kind=kOutput, calls=%fused_computation.4 | convolution fusion | flops 868208640 | bytes 103121920 | tf_op jit(solution)/shard_map/qhd,khd->hqk/dot_general | solution.py:113
  813.3 42.5 %multiply_convert_fusion.1 = (bf16[12,512,1024]{2,1,0:T(8,128)(2,1)}, bf16[12,512,1024]{2,1,0:T(8,128)(2,1)}) fusion(f32[12,512,1024]{2,1,0:T(8,128)} %get-tuple-element.279, f32[12,512]{1,0:T(8,128)S(1)} %get-tuple-element.214, f32[12,512]{1,0:T(8,128)S(1)} %get-tuple-element.287, f32[12,512,1024]{2,1,0:T(8,128)} %get-tuple-element.266, ...), kind=kLoop, calls=%fused_computation.3 | loop fusion | flops 75497472 | bytes 125928448 | tf_op jit(solution)/shard_map/convert_element_type | solution.py:117
  937.2 113.0 %all-to-all-done.1 = bf16[16,48,3073]{2,1,0:T(8,128)(2,1)} async-done(((bf16[16,48,3073]{2,1,0:T(8,128)(2,1)}), bf16[16,48,3073]{2,1,0:T(8,128)(2,1)}, u32[]{:S(2)}, u32[]{:S(2)}) %all-to-all-start.1) | async-done | bytes 4720160 | tf_op jit(solution)/shard_map/all_to_all | solution.py:23
  1056.0 126.2 %reduce-scatter.11.cloned.1.call-done = f32[192,768]{1,0:T(8,128)} async-done(((f32[3072,768]{1,0:T(8,128)}), f32[192,768]{1,0:T(8,128)}) %reduce-scatter.11.cloned.1.call-update) | async-done | bytes 589840 | tf_op jit(solution)/shard_map/reduce_scatter | solution.py:321
  1184.0 173.9 %reduce-scatter.9.cloned.1.call-done = f32[48,3072]{1,0:T(8,128)} async-done(((f32[768,3072]{1,0:T(8,128)}), f32[48,3072]{1,0:T(8,128)}) %reduce-scatter.9.cloned.1.call-update) | async-done | bytes 589840 | tf_op jit(solution)/shard_map/reduce_scatter | solution.py:320
  1373.3 77.1 %all-reduce.12 = (bf16[768]{0:T(1024)(128)(2,1)S(1)}, bf16[768]{0:T(1024)(128)(2,1)S(1)}, bf16[768]{0:T(1024)(128)(2,1)S(1)}, bf16[768]{0:T(1024)(128)(2,1)S(1)}) all-reduce(f32[768]{0:T(1024)S(1)} %get-tuple-element.291, f32[768]{0:T(1024)S(1)} %get-tuple-element.290, ...), channel_id=2, replica_groups=mesh['fsdp'=16,'rep'=2] {'fsdp'}, use_global_device_ids=true, to_apply=%region_35.36.clone | all-reduce | flops 3072 | bytes 18432
  (414 shorter events, 393.4 us)
Async XLA Ops:
  7.2 100.5 %all-gather.11.cloned.1.call-start = ((), (), s32[]{:S(2)}) async-start(), calls=%async_computation.7 | async-start | bytes 1253376 | tf_op jit(solution)/shard_map/all_gather | solution.py:235
  7.9 119.6 %all-gather.13.cloned.1.call-start = ((), (), s32[]{:S(2)}) async-start(), calls=%async_computation.8 | async-start | bytes 1253376 | tf_op jit(solution)/shard_map/all_gather | solution.py:236
  8.7 176.7 %all-gather.9.cloned.1.call-start = ((), (), s32[]{:S(2)}) async-start(), calls=%async_computation.6 | async-start | bytes 1253376 | tf_op jit(solution)/shard_map/all_gather | solution.py:237
  9.4 233.7 %all-gather.15.cloned.1.call-start = ((), (), s32[]{:S(2)}) async-start(), calls=%async_computation.9 | async-start | bytes 1253376 | tf_op jit(solution)/shard_map/all_gather | solution.py:238
  10.0 305.9 %all-gather.17.cloned.1.call-start = ((), (), s32[]{:S(2)}) async-start(), calls=%async_computation.10 | async-start | bytes 3760128 | tf_op jit(solution)/shard_map/all_gather | solution.py:244
  10.6 380.2 %all-gather.19.cloned.1.call-start = ((), (), s32[]{:S(2)}) async-start(), calls=%async_computation.11 | async-start | bytes 1253376 | tf_op jit(solution)/shard_map/all_gather | solution.py:245
  11.2 444.3 %all-gather.21.cloned.1.call-start = ((), (), s32[]{:S(2)}) async-start(), calls=%async_computation.12 | async-start | bytes 5013504 | tf_op jit(solution)/shard_map/all_gather | solution.py:248
  11.9 525.4 %all-gather.23.cloned.1.call-start = ((), (), s32[]{:S(2)}) async-start(), calls=%async_computation.13 | async-start | bytes 5013504 | tf_op jit(solution)/shard_map/all_gather | solution.py:249
  12.7 923.0 %reduce-scatter.7.cloned.1.call-start = ((), (), s32[]{:S(2)}) async-start(), calls=%async_computation.15 | async-start | bytes 2506752 | tf_op jit(solution)/shard_map/reduce_scatter | solution.py:317
  14.0 186.8 %copy-start.86 = (pred[1024]{0:T(1024)(128)(4,1)}, pred[1024]{0:T(1024)(128)(4,1)S(1)}, u32[]{:S(2)}) copy-start(pred[1024]{0:T(1024)(128)(4,1)S(1)} %iota_compare_fusion.2) | copy-start | bytes 3076
  100.0 215.9 %copy-start.72 = (f32[768]{0:T(1024)}, f32[768]{0:T(1024)S(1)}, u32[]{:S(2)}) copy-start(f32[768]{0:T(1024)S(1)} %convert_element_type.288) | copy-start | bytes 9220
  100.6 215.3 %copy-start.94 = (f32[768]{0:T(1024)}, f32[768]{0:T(1024)S(1)}, u32[]{:S(2)}) copy-start(f32[768]{0:T(1024)S(1)} %convert_element_type.289) | copy-start | bytes 9220
  394.9 173.1 %copy-start.50 = (f32[1024]{0:T(1024)}, f32[1024]{0:T(1024)S(1)}, u32[]{:S(2)}) copy-start(f32[1024]{0:T(1024)S(1)} %broadcast_multiply_fusion.4) | copy-start | bytes 12292
  397.5 170.5 %copy-start.54 = (f32[1024]{0:T(1024)}, f32[1024]{0:T(1024)S(1)}, u32[]{:S(2)}) copy-start(f32[1024]{0:T(1024)S(1)} %fusion.81) | copy-start | bytes 12292
  624.3 429.9 %reduce-scatter.5.cloned.1.call-start = ((), (), s32[]{:S(2)}) async-start(), calls=%async_computation.14 | async-start | bytes 7520256 | tf_op jit(solution)/shard_map/reduce_scatter | solution.py:316
  689.1 493.1 %reduce-scatter.11.cloned.1.call-start = ((), (), s32[]{:S(2)}) async-start(), calls=%async_computation.17 | async-start | bytes 10027008 | tf_op jit(solution)/shard_map/reduce_scatter | solution.py:321
  703.5 654.4 %reduce-scatter.9.cloned.1.call-start = ((), (), s32[]{:S(2)}) async-start(), calls=%async_computation.16 | async-start | bytes 10027008 | tf_op jit(solution)/shard_map/reduce_scatter | solution.py:320
  910.4 139.8 %all-to-all-start.1 = ((bf16[16,48,3073]{2,1,0:T(8,128)(2,1)}), bf16[16,48,3073]{2,1,0:T(8,128)(2,1)}, u32[]{:S(2)}, u32[]{:S(2)}) async-start(bf16[16,48,3073]{2,1,0:T(8,128)(2,1)} %concatenate.65), calls=%async_computation.1 | async-start | bytes 9830400 | tf_op jit(solution)/shard_map/all_to_all | solution.py:23
  915.1 544.9 %all-reduce.18.cloned.1.call-start = ((), (), s32[]{:S(2)}) async-start(), calls=%async_computation.18 | async-start | bytes 2359296 | tf_op jit(solution)/shard_map/psum | solution.py:377
  1056.0 311.6 %copy-start.85 = (f32[768]{0:T(1024)S(1)}, f32[768]{0:T(1024)}, u32[]{:S(2)}) copy-start(f32[768]{0:T(1024)} %get-tuple-element.210) | copy-start | bytes 9220
  1056.0 311.6 %copy-start.96 = (f32[768]{0:T(1024)S(1)}, f32[768]{0:T(1024)}, u32[]{:S(2)}) copy-start(f32[768]{0:T(1024)} %get-tuple-element.284) | copy-start | bytes 9220
  1056.0 311.6 %copy-start.84 = (f32[768]{0:T(1024)S(1)}, f32[768]{0:T(1024)}, u32[]{:S(2)}) copy-start(f32[768]{0:T(1024)} %get-tuple-element.208) | copy-start | bytes 9220
  1056.0 311.6 %copy-start.97 = (f32[768]{0:T(1024)S(1)}, f32[768]{0:T(1024)}, u32[]{:S(2)}) copy-start(f32[768]{0:T(1024)} %get-tuple-element.282) | copy-start | bytes 9220
  1363.0 91.2 %all-to-all-start = ((bf16[16,1,48]{2,1,0:T(2,128)(2,1)}), bf16[16,1,48]{2,1,0:T(2,128)(2,1)S(1)}, u32[]{:S(2)}, u32[]{:S(2)}) async-start(bf16[16,1,48]{2,1,0:T(2,128)(2,1)} %convert_element_type.356), calls=%async_computation | async-start | bytes 16384 | tf_op jit(solution)/shard_map/all_to_all | solution.py:23
  (105 other events, 1769.9 us)
Sparse Core Ops, SparseCore 0:
  10.8 59.1 all-gather.10
  72.8 54.7 all-gather.12
  130.4 54.9 all-gather.8
  188.1 55.0 all-gather.14
  245.8 70.1 all-gather.16
  318.6 54.6 all-gather.18
  376.1 79.3 all-gather.20
  458.2 79.0 all-gather.22
  624.5 127.1 reduce-scatter.6
  757.7 150.5 reduce-scatter.4
  914.9 267.2 reduce-scatter.10
  1187.7 170.1 reduce-scatter.8
  1362.2 18.9 all-reduce.17
where the time goes:
time: 1490 us; the launch traced here: 1480 us
  waiting for transfers between devices  669 us (45%)
  matrix products  372 us (25%)
  other arithmetic  166 us (11%)
  blocking collectives  158 us (11%)
  local copies, waits for them, and re-layouts  86.3 us (6%)
  between operations  18.4 us (1%)
    reduce_scatter x1, waiting for transfers between devices, shards(): lax.psum_scatter(block_terms[6], 'fsdp', scatter_dimension=0, tiled=True)  174 us
    unnamed x2, blocking collectives  156 us
    reduce_scatter x1, waiting for transfers between devices, shards(): lax.psum_scatter(block_terms[7], 'fsdp', scatter_dimension=0, tiled=True)  126 us
    all_to_all x2, waiting for transfers between devices, sum_at_owner(): lax.all_to_all(tiles, axis, split_axis=0, concat_axis=0, tiled=True)  113 us
    convert_element_type x3, other arithmetic, attend_back(): grad_scores = (chances * (grad_probs - inner_sum)).astype(jnp.bfloat16)  74.7 us
    dot_general x4, matrix products, attend_back(): jnp.einsum('qhd,khd->hqk', grad_block, value_block, preferred_element_typ...  72.3 us
    all_gather x1, waiting for transfers between devices, shards(): lax.all_gather(mlp_down, 'fsdp', axis=0, tiled=True)  70.8 us
    all_gather x1, waiting for transfers between devices, shards(): lax.all_gather(attn_qkv, 'fsdp', axis=0, tiled=True)  67.4 us
  transfers between devices with their start and end apart: 15, of which 9 were waited for; matrix products, arithmetic and copies ran while one was open for 34% of the time, Pallas kernels for 0%

commit v1 on v0

v1 whole, which is shorter than its diff:
```python
import functools

import jax
import jax.numpy as jnp
from jax import lax
from jax.experimental import pallas as pl
from jax.experimental.pallas import tpu as pltpu
from jax.sharding import PartitionSpec as P

D = 768
FRAME_TOK = 256
EPS = 1e-05
MESH = pl.DeviceIdType.MESH

F32, BF16 = jnp.float32, jnp.bfloat16
NN = (((1,), (0,)), ((), ()))
NT = (((1,), (1,)), ((), ()))
TN = (((0,), (0,)), ((), ()))
def dg(a, b, dims): return lax.dot_general(a, b, dims, preferred_element_type=F32)

def head_sides(side, q2, k2, bias):
    lane = lax.broadcasted_iota(jnp.int32, (1, 128), 1)
    mine = (lane >= 64) if side else (lane < 64)
    extra = lane == (0 if side else 64)
    qa = jnp.where(mine, q2, jnp.where(extra, 1.0, 0.0).astype(BF16))
    ka = jnp.where(mine, k2, jnp.where(extra, bias, 0.0).astype(BF16))
    return qa, ka

def fwd_kernel(n_ref, q_ref, k_ref, v_ref, o_ref, l_ref, vt, *, causal, bq, unit):
    T = q_ref.shape[0]; K = k_ref.shape[0]
    live = n_ref[0] * unit
    bias = jnp.where(lax.broadcasted_iota(jnp.int32, (K, 1), 0) < live, 0.0, -1e30).astype(F32)
    q2 = q_ref[...] * BF16(0.125)
    k2 = k_ref[...]
    vt[...] = v_ref[...].T
    for side in range(2):
        qa, ka = head_sides(side, q2, k2, bias)
        for j in range(T // bq):
            span = (j + 1) * bq if causal else K
            s = dg(ka[:span], qa[j * bq:(j + 1) * bq], NT)
            if causal:
                top = j * bq
                diag = s[top:]
                ok = lax.broadcasted_iota(jnp.int32, (bq, bq), 0) <= lax.broadcasted_iota(jnp.int32, (bq, bq), 1)
                diag = jnp.where(ok, diag, -1e30)
                s = diag if top == 0 else jnp.concatenate([s[:top], diag], 0)
            m = jnp.max(s, 0, keepdims=True)
            p = jnp.exp(s - m)
            l = jnp.sum(p, 0, keepdims=True)
            ot = dg(vt[side * 64:(side + 1) * 64, :span], p.astype(BF16), NN) * (1.0 / l)
            o_ref[j * bq:(j + 1) * bq, side * 64:(side + 1) * 64] = ot.T.astype(BF16)
            l_ref[0, side:side + 1, j * bq:(j + 1) * bq] = m + jnp.log(l)

def attn_fwd(live, q, k, v, qo, ko, vo, causal, unit, bq=256):
    T, K = q.shape[0], k.shape[0]
    G = 6
    return pl.pallas_call(functools.partial(fwd_kernel, causal=causal, bq=bq, unit=unit),
        grid=(G,),
        in_specs=[pl.BlockSpec(memory_space=pltpu.SMEM), pl.BlockSpec((T, 128), lambda i: (0, i + qo)), pl.BlockSpec((K, 128), lambda i: (0, i + ko)), pl.BlockSpec((K, 128), lambda i: (0, i + vo))],
        out_specs=[pl.BlockSpec((T, 128), lambda i: (0, i)), pl.BlockSpec((1, 2, T), lambda i: (i, 0, 0))],
        out_shape=[jax.ShapeDtypeStruct((T, 768), BF16), jax.ShapeDtypeStruct((G, 2, T), F32)],
        scratch_shapes=[pltpu.VMEM((128, K), BF16)],
        compiler_params=pltpu.CompilerParams(vmem_limit_bytes=48 << 20), name="attn_fwd")(live, q, k, v)

def bwd_kernel(n_ref, q_ref, k_ref, v_ref, o_ref, do_ref, l_ref, g_ref, kt, dqt, dka, dva, *, causal, bq, bk, unit):
    T = q_ref.shape[0]; K = k_ref.shape[0]
    live = n_ref[0] * unit
    bias = jnp.where(lax.broadcasted_iota(jnp.int32, (K, 1), 0) < live, 0.0, -1e30).astype(F32)
    q2 = q_ref[...] * BF16(0.125)
    k2 = k_ref[...]; v2 = v_ref[...]
    do2 = do_ref[...]
    kt[...] = k2.T
    prod = (do2.astype(F32) * o_ref[...].astype(F32)).T
    lane = lax.broadcasted_iota(jnp.int32, (1, 128), 1)
    for side in range(2):
        qa, ka = head_sides(side, q2, k2, bias)
        mine = (lane >= 64) if side else (lane < 64)
        va = jnp.where(mine, v2, BF16(0))
        delta = jnp.sum(prod[side * 64:(side + 1) * 64], 0, keepdims=True)
        lse = l_ref[0, side:side + 1, :]
        for i in range(K // bk):
            dk = dv = None
            kb, vb = ka[i * bk:(i + 1) * bk], va[i * bk:(i + 1) * bk]
            for j in range(T // bq):
                if causal and (j + 1) * bq <= i * bk: continue
                cols = slice(j * bq, (j + 1) * bq)
                s = dg(kb, qa[cols], NT)
                p = jnp.exp(s - lse[:, cols])
                if causal and j * bq < (i + 1) * bk:
                    ok = i * bk + lax.broadcasted_iota(jnp.int32, (bk, bq), 0) <= j * bq + lax.broadcasted_iota(jnp.int32, (bk, bq), 1)
                    p = jnp.where(ok, p, 0.0)
                dp = dg(vb, do2[cols], NT)
                ds = (p * (dp - delta[:, cols])).astype(BF16)
                a = dg(p.astype(BF16), do2[cols], NN)
                b = dg(ds, q2[cols], NN)
                dv = a if dv is None else dv + a
                dk = b if dk is None else dk + b
                c = dg(kt[side * 64:(side + 1) * 64, i * bk:(i + 1) * bk], ds, NN)
                if i == 0: dqt[side * 64:(side + 1) * 64, cols] = c
                else: dqt[side * 64:(side + 1) * 64, cols] += c
            rows = slice(i * bk, (i + 1) * bk)
            if side == 0:
                dka[rows] = dk; dva[rows] = dv
            else:
                g_ref[1, rows, :] = jnp.where(lane < 64, dka[rows], dk).astype(BF16)
                g_ref[2, rows, :] = jnp.where(lane < 64, dva[rows], dv).astype(BF16)
    g_ref[0] = (dqt[...] * 0.125).T.astype(BF16)

def attn_bwd(live, q, k, v, o, do, lse, qo, ko, vo, causal, unit, bq=256, bk=256):
    T, K = q.shape[0], k.shape[0]
    G = 6
    return pl.pallas_call(functools.partial(bwd_kernel, causal=causal, bq=bq, bk=bk, unit=unit),
        grid=(G,),
        in_specs=[pl.BlockSpec(memory_space=pltpu.SMEM), pl.BlockSpec((T, 128), lambda i: (0, i + qo)), pl.BlockSpec((K, 128), lambda i: (0, i + ko)), pl.BlockSpec((K, 128), lambda i: (0, i + vo)),
                  pl.BlockSpec((T, 128), lambda i: (0, i)), pl.BlockSpec((T, 128), lambda i: (0, i)), pl.BlockSpec((1, 2, T), lambda i: (i, 0, 0))],
        out_specs=pl.BlockSpec((3, T, 128), lambda i: (0, 0, i)),
        out_shape=jax.ShapeDtypeStruct((3, T, 768), BF16),
        scratch_shapes=[pltpu.VMEM((128, K), BF16), pltpu.VMEM((128, T), F32), pltpu.VMEM((K, 128), F32), pltpu.VMEM((K, 128), F32)],
        compiler_params=pltpu.CompilerParams(vmem_limit_bytes=48 << 20), name="attn_bwd")(live, q, k, v, o, do, lse)


def grid_of(n):
    if n == 16:
        return 4, 2, 2
    if n == 64:
        return 4, 4, 4
    return n, 1, 1


def pieces_of(shards):
    out = []
    for i, s in enumerate(shards):
        rows, cols = s
        step = 256 if rows > cols // 8 and cols == 768 else min(cols, 768)
        out += [(i, c, step) for c in range(0, cols, step)]
    return out


class Place:
    def __init__(self, dims):
        self.Z, self.Y, self.X = dims
        self.me = lax.axis_index("fsdp")
        self.core = lax.axis_index("rep")
        self.z = self.me // (self.Y * self.X)
        self.y = (self.me // self.X) % self.Y
        self.x = self.me % self.X

    def at(self, z, y, x):
        return ((z * self.Y + y) * self.X + x, self.core)

    def peers(self, axis):
        count = {"z": self.Z, "y": self.Y, "x": self.X}[axis]
        mine = {"z": self.z, "y": self.y, "x": self.x}[axis]
        out = []
        for k in range(1, count):
            there = (mine + k) % count
            at = {"z": self.z, "y": self.y, "x": self.x}
            at[axis] = there
            out.append((there, (mine + count - k) % count, self.at(at["z"], at["y"], at["x"])))
        return out

    def sibling(self):
        return (self.me, 1 - self.core)

    def greet(self):
        bar = pltpu.get_barrier_semaphore()
        devs = [d for axis in "zyx" for _, _, d in self.peers(axis)] + [self.sibling()]
        for d in devs:
            pl.semaphore_signal(bar, inc=1, device_id=d, device_id_type=MESH)
        pl.semaphore_wait(bar, len(devs))


def remote(src, dst, send, recv, dev):
    return pltpu.make_async_remote_copy(
        src_ref=src, dst_ref=dst, send_sem=send, recv_sem=recv, device_id=dev, device_id_type=MESH
    )


def gather_kernel(*refs, dims, pieces, count):
    shards, outs = refs[:count], refs[count : 2 * count]
    own_sem, s1, r1, s2, r2, s3, r3, t1, u1, t2, u2, t3, u3 = refs[2 * count :]
    pl_ = Place(dims)
    Z, Y, X = dims
    pl_.greet()
    own = [
        pltpu.make_async_copy(shards[i], outs[i].at[pl_.z, pl_.y, pl_.x], own_sem.at[i])
        for i in range(count)
    ]
    for c in own:
        c.start()

    def both_ways(core, a, b):
        mine = {"z": pl_.z, "y": pl_.y, "x": pl_.x}

        def span(m, side):
            i, c, w = pieces[m]
            return pl.ds(c + side * (w // 2), w // 2)

        def view(m, side, z=None, y=None, x=None):
            i = pieces[m][0]
            every = slice(None)
            return outs[i].at[
                every if z is None else z,
                every if y is None else y,
                every if x is None else x,
                every,
                span(m, side),
            ]

        def first(m):
            i = pieces[m][0]
            for k, (_, _, dev) in enumerate(pl_.peers("z")):
                src = shards[i].at[:, span(m, core)]
                yield remote(src, view(m, core, pl_.z, pl_.y, pl_.x), s1.at[m, k], r1.at[m, k], dev)

        def first_here(m):
            for k, (_, frm, dev) in enumerate(pl_.peers("z")):
                dst = view(m, core, frm, pl_.y, pl_.x)
                yield remote(dst, dst, s1.at[m, k], r1.at[m, k], dev), dst, (frm, pl_.y, pl_.x)

        def second(m, start):
            for k, (_, frm, dev) in enumerate(pl_.peers(a)):
                at = dict(y=pl_.y, x=pl_.x)
                if not start:
                    at[a] = frm
                v = view(m, core, None, at["y"], at["x"])
                yield remote(v, v, s2.at[m, k], r2.at[m, k], dev), (None, at["y"], at["x"])

        def third(m, start):
            for k, (_, frm, dev) in enumerate(pl_.peers(b)):
                at = {a: None, b: mine[b] if start else frm}
                v = view(m, core, None, at["y"], at["x"])
                yield remote(v, v, s3.at[m, k], r3.at[m, k], dev), (None, at["y"], at["x"])

        def give(m, k, where, sem_s, sem_r):
            v = view(m, core, *where)
            return remote(v, v, sem_s.at[m, k], sem_r.at[m, k], pl_.sibling())

        M = len(pieces)
        sent = []
        for m in range(M):
            for c in first(m):
                c.start()
                sent.append(c)
        for c in own:
            c.wait()
        for t in range(M + 2):
            if t < M:
                for k, (c, _, where) in enumerate(first_here(t)):
                    c.wait_recv()
                for c, _ in second(t, True):
                    c.start()
                    sent.append(c)
                for k, (c, _, where) in enumerate(first_here(t)):
                    g = give(t, k, where, t1, u1)
                    g.start()
                    sent.append(g)
            m = t - 1
            if 0 <= m < M:
                got = list(second(m, False))
                for c, _ in got:
                    c.wait_recv()
                for c, _ in third(m, True):
                    c.start()
                    sent.append(c)
                for k, (_, where) in enumerate(got):
                    g = give(m, k, where, t2, u2)
                    g.start()
                    sent.append(g)
            m = t - 2
            if 0 <= m < M:
                got = list(third(m, False))
                for c, _ in got:
                    c.wait_recv()
                for k, (_, where) in enumerate(got):
                    g = give(m, k, where, t3, u3)
                    g.start()
                    sent.append(g)
        for c in sent:
            c.wait_send()
        for m in range(M):
            def come(k, where, sem_s, sem_r):
                v = view(m, 1 - core, *where)
                remote(v, v, sem_s.at[m, k], sem_r.at[m, k], pl_.sibling()).wait_recv()

            for k, (_, frm, _) in enumerate(pl_.peers("z")):
                come(k, (frm, pl_.y, pl_.x), t1, u1)
            for k, (_, frm, _) in enumerate(pl_.peers(b)):
                at = dict(y=pl_.y, x=pl_.x)
                at[b] = frm
                come(k, (None, at["y"], at["x"]), t2, u2)
            for k, (_, frm, _) in enumerate(pl_.peers(a)):
                at = {b: None, a: frm}
                come(k, (None, at["y"], at["x"]), t3, u3)

    @pl.when(pl_.core == 0)
    def _():
        both_ways(0, "x", "y")

    @pl.when(pl_.core == 1)
    def _():
        both_ways(1, "y", "x")


def gather_all(shards, n):
    dims = grid_of(n)
    Z, Y, X = dims
    pieces = pieces_of([s.shape for s in shards])
    M, count = len(pieces), len(shards)
    side = max(Y, X) - 1
    sem = pltpu.SemaphoreType.DMA
    counts = [max(Z - 1, 1)] * 2 + [max(side, 1)] * 4 + [max(Z - 1, 1)] * 2 + [max(side, 1)] * 4
    any_ = pl.BlockSpec(memory_space=pl.ANY)
    outs = pl.pallas_call(
        functools.partial(gather_kernel, dims=dims, pieces=pieces, count=count),
        out_shape=[jax.ShapeDtypeStruct((Z, Y, X) + s.shape, s.dtype) for s in shards],
        in_specs=[any_] * count,
        out_specs=[any_] * count,
        scratch_shapes=[sem((count,))] + [sem((M, c)) for c in counts],
        compiler_params=pltpu.CompilerParams(collective_id=0, has_side_effects=True),
        name="gather_weights",
    )(*shards)
    return [o.reshape((n,) + s.shape) for o, s in zip(outs, shards)]


def scatter_kernel(*refs, dims, pieces, count, groups, scale):
    grads, outs = refs[:count], refs[count : count + groups]
    (acc, sib, got1, got2, got3, half, lsem, s0, r0, s1, r1, s2, r2, s3, r3, s4, r4, osem) = refs[
        count + groups :
    ]
    pl_ = Place(dims)
    Z, Y, X = dims
    pl_.greet()

    def both_ways(core, a, b):
        size = {"y": Y, "x": X}
        mine = {"y": pl_.y, "x": pl_.x}
        A, B = size[a], size[b]

        def chunk(m, side, y, x):
            i, c, w, _, _ = pieces[m]
            return grads[i].at[:, y, x, :, pl.ds(c + side * (w // 2), w // 2)]

        def order(core_, y, x):
            return (y, x) if core_ == 0 else (x, y)

        def stage0(m):
            for y in range(Y):
                for x in range(X):
                    k = y * X + x
                    p, q = order(core, y, x)
                    yield pltpu.make_async_copy(chunk(m, core, y, x), acc[m].at[p, q], lsem.at[m, k])
                    p, q = order(1 - core, y, x)
                    yield remote(
                        chunk(m, 1 - core, y, x), sib[m].at[p, q], s0.at[m, k], r0.at[m, k], pl_.sibling()
                    )

        def add(dst, *srcs):
            total = dst[...].astype(F32)
            for s in srcs:
                total = total + s[...].astype(F32)
            dst[...] = total.astype(BF16)

        def stage1(m):
            for k, (there, _, dev) in enumerate(pl_.peers(b)):
                yield remote(acc[m].at[there], got1[m].at[k], s1.at[m, k], r1.at[m, k], dev)

        def stage2(m):
            for k, (there, _, dev) in enumerate(pl_.peers(a)):
                yield remote(acc[m].at[mine[b], there], got2[m].at[k], s2.at[m, k], r2.at[m, k], dev)

        def stage3(m):
            for k, (there, _, dev) in enumerate(pl_.peers("z")):
                yield remote(
                    acc[m].at[mine[b], mine[a], there], got3[m].at[k], s3.at[m, k], r3.at[m, k], dev
                )

        def stage4(m):
            yield remote(half[m].at[core], half[m].at[core], s4.at[m], r4.at[m], pl_.sibling())

        M = len(pieces)
        for m in range(M):
            for c in stage0(m):
                c.start()
        sent = []
        for t in range(M + 4):
            if t < M:
                m = t
                for c in stage0(m):
                    c.wait()
                for j in range(B):
                    add(acc[m].at[j], sib[m].at[j])
                for c in stage1(m):
                    c.start()
                    sent.append(c)
            m = t - 1
            if 0 <= m < M:
                for c in stage1(m):
                    c.wait_recv()
                add(acc[m].at[mine[b]], *[got1[m].at[k] for k in range(B - 1)])
                for c in stage2(m):
                    c.start()
                    sent.append(c)
            m = t - 2
            if 0 <= m < M:
                for c in stage2(m):
                    c.wait_recv()
                add(acc[m].at[mine[b], mine[a]], *[got2[m].at[k] for k in range(A - 1)])
                for c in stage3(m):
                    c.start()
                    sent.append(c)
            m = t - 3
            if 0 <= m < M:
                for c in stage3(m):
                    c.wait_recv()
                total = acc[m][mine[b], mine[a], pl_.z].astype(F32)
                for k in range(Z - 1):
                    total = total + got3[m][k].astype(F32)
                half[m][core] = total * scale
                for c in stage4(m):
                    c.start()
                    sent.append(c)
        for c in sent:
            c.wait_send()
        for m in range(M):
            theirs = half[m].at[1 - core]
            remote(theirs, theirs, s4.at[m], r4.at[m], pl_.sibling()).wait_recv()
            i, c, w, o, oc = pieces[m]
            for side in range(2):
                outs[o][:, oc + side * (w // 2) : oc + (side + 1) * (w // 2)] = half[m][side]

    @pl.when(pl_.core == 0)
    def _():
        both_ways(0, "x", "y")

    @pl.when(pl_.core == 1)
    def _():
        both_ways(1, "y", "x")


def scatter_all(grads, targets, n, scale):
    dims = grid_of(n)
    Z, Y, X = dims
    grads = [g.reshape((Z, Y, X) + g.shape[1:]) for g in grads]
    pieces = [
        (i, c, w, targets[i][0], targets[i][1] + c)
        for i, c, w in pieces_of([g.shape[3:] for g in grads])
    ]
    groups = 1 + max(t[0] for t in targets)
    widths = [0] * groups
    rows = [0] * groups
    for g, (o, c) in zip(grads, targets):
        widths[o] = max(widths[o], c + g.shape[4])
        rows[o] = g.shape[3]
    M, count = len(pieces), len(grads)
    S = max(Y, X)
    sem = pltpu.SemaphoreType.DMA
    any_ = pl.BlockSpec(memory_space=pl.ANY)
    vm = pl.BlockSpec(memory_space=pltpu.VMEM)
    shape = [(grads[i].shape[3], w // 2) for i, _, w, _, _ in pieces]
    one = max(S - 1, 1)
    return pl.pallas_call(
        functools.partial(
            scatter_kernel, dims=dims, pieces=pieces, count=count, groups=groups, scale=scale
        ),
        out_shape=[jax.ShapeDtypeStruct((r, w), F32) for r, w in zip(rows, widths)],
        in_specs=[any_] * count,
        out_specs=[vm] * groups,
        scratch_shapes=[
            [pltpu.VMEM((S, S, Z) + s, BF16) for s in shape],
            [pltpu.VMEM((S, S, Z) + s, BF16) for s in shape],
            [pltpu.VMEM((one, S, Z) + s, BF16) for s in shape],
            [pltpu.VMEM((one, Z) + s, BF16) for s in shape],
            [pltpu.VMEM((max(Z - 1, 1),) + s, BF16) for s in shape],
            [pltpu.VMEM((2,) + s, F32) for s in shape],
        ]
        + [sem((M, S * S))] * 3
        + [sem((M, one))] * 4
        + [sem((M, max(Z - 1, 1)))] * 2
        + [sem((M,))] * 3,
        compiler_params=pltpu.CompilerParams(
            collective_id=1, has_side_effects=True, vmem_limit_bytes=58 << 20
        ),
        name="scatter_grads",
    )(*grads)


def moments(values):
    average = jnp.mean(values, -1, keepdims=True)
    centred = values - average
    variance = jnp.mean(centred * centred, -1, keepdims=True)
    inverse = lax.rsqrt(variance + EPS)
    return centred * inverse, inverse


def norm_back(normal, inverse, gain, grad):
    m = grad * gain
    back = inverse * (
        m - jnp.mean(m, -1, keepdims=True) - normal * jnp.mean(m * normal, -1, keepdims=True)
    )
    return back, jnp.sum(grad * normal, 0), jnp.sum(grad, 0)


GELU_A = 0.7978845608028654
GELU_B = 0.044715


def gelu(u):
    return 0.5 * u * (1.0 + jnp.tanh(GELU_A * (u + GELU_B * u * u * u)))


def gelu_slope(u):
    t = jnp.tanh(GELU_A * (u + GELU_B * u * u * u))
    return 0.5 * (1.0 + t) + 0.5 * u * (1.0 - t * t) * (GELU_A * (1.0 + 3.0 * GELU_B * u * u))


def shards(
    tokens,
    context,
    clip_lengths,
    context_frames,
    norm1_gain,
    norm1_bias,
    cross_q,
    cross_k,
    cross_v,
    cross_out,
    norm2_gain,
    norm2_bias,
    attn_qkv,
    attn_out,
    norm3_gain,
    norm3_bias,
    mlp_up,
    mlp_down,
    cotangent,
):
    n = lax.axis_size("fsdp")
    stream_in = tokens[0].astype(F32)
    context_rows = context[0]
    slot_rows = stream_in.shape[0]
    own = norm1_gain.shape[0]
    padding = (jnp.arange(slot_rows) < clip_lengths[0])[:, None]
    norms = jnp.stack([norm1_gain, norm1_bias, norm2_gain, norm2_bias, norm3_gain, norm3_bias])
    norms = jnp.pad(norms, ((0, 10), (0, 256 - own)))
    whole = gather_all(
        [norms, cross_q, cross_k, cross_v, cross_out, attn_qkv, attn_out, mlp_up, mlp_down], n
    )
    norms = whole[0][:, :6, :own].transpose(1, 0, 2).reshape(6, D).astype(F32)
    gain_one, bias_one, gain_two, bias_two, gain_three, bias_three = [norms[i] for i in range(6)]
    w_q, w_k, w_v, w_o, w_qkv, w_p, w_up, w_down = [
        w.reshape(-1, w.shape[2]) for w in whole[1:]
    ]

    normal_one, inverse_one = moments(stream_in)
    h1 = (normal_one * gain_one + bias_one).astype(BF16)
    q1 = dg(h1, w_q, NN).astype(BF16)
    k1 = dg(context_rows, w_k, NN).astype(BF16)
    v1 = dg(context_rows, w_v, NN).astype(BF16)
    o1, lse1 = attn_fwd(context_frames, q1, k1, v1, 0, 0, 0, False, FRAME_TOK, 512)
    x1 = stream_in + dg(o1, w_o, NN)
    normal_two, inverse_two = moments(x1)
    h2 = (normal_two * gain_two + bias_two).astype(BF16)
    qkv = dg(h2, w_qkv, NN).astype(BF16)
    o2, lse2 = attn_fwd(clip_lengths, qkv, qkv, qkv, 0, 6, 12, True, 1, 512)
    x2 = x1 + dg(o2, w_p, NN)
    normal_three, inverse_three = moments(x2)
    h3 = (normal_three * gain_three + bias_three).astype(BF16)
    up = dg(h3, w_up, NN)
    hidden = gelu(up).astype(BF16)
    x3 = x2 + dg(hidden, w_down, NN)
    block_out = jnp.where(padding, x3, 0.0).astype(BF16)

    dx3 = jnp.where(padding, cotangent[0].astype(F32), 0.0)
    dz = dx3.astype(BF16)
    dup = (dg(dz, w_down, NT) * gelu_slope(up)).astype(BF16)
    back, g_gain3, g_bias3 = norm_back(normal_three, inverse_three, gain_three, dg(dup, w_up, NT))
    dx2 = dx3 + back
    dy2 = dx2.astype(BF16)
    do2 = dg(dy2, w_p, NT).astype(BF16)
    dqkv = attn_bwd(clip_lengths, qkv, qkv, qkv, o2, do2, lse2, 0, 6, 12, True, 1, 256, 512)
    dh2 = sum(dg(dqkv[c], w_qkv[:, c * D : (c + 1) * D], NT) for c in range(3))
    back, g_gain2, g_bias2 = norm_back(normal_two, inverse_two, gain_two, dh2)
    dx1 = dx2 + back
    dy1 = dx1.astype(BF16)
    do1 = dg(dy1, w_o, NT).astype(BF16)
    dqkv1 = attn_bwd(context_frames, q1, k1, v1, o1, do1, lse1, 0, 0, 0, False, FRAME_TOK, 1024, 256)
    dh1 = dg(dqkv1[0], w_q, NT)
    back, g_gain1, g_bias1 = norm_back(normal_one, inverse_one, gain_one, dh1)
    input_grad = dx1 + back

    g_norms = jnp.stack([g_gain1, g_bias1, g_gain2, g_bias2, g_gain3, g_bias3]).astype(BF16)
    g_norms = jnp.pad(g_norms.reshape(6, n, own).transpose(1, 0, 2), ((0, 0), (0, 10), (0, 256 - own)))

    def weight(left, right):
        g = dg(left, right, TN).astype(BF16)
        return g.reshape(n, -1, g.shape[1])

    grads = [
        (weight(hidden, dz), (8, 0)),
        (weight(h3, dup), (7, 0)),
        (weight(o2, dy2), (6, 0)),
        (weight(h2, dqkv[0]), (5, 0)),
        (weight(h2, dqkv[1]), (5, D)),
        (weight(h2, dqkv[2]), (5, 2 * D)),
        (weight(o1, dy1), (4, 0)),
        (weight(context_rows, dqkv1[2]), (3, 0)),
        (weight(context_rows, dqkv1[1]), (2, 0)),
        (weight(h1, dqkv1[0]), (1, 0)),
        (g_norms, (0, 0)),
    ]
    scale = (slot_rows * tokens.shape[0] * n * lax.axis_size("rep")) ** (-0.5)
    done = scatter_all([g for g, _ in grads], [t for _, t in grads], n, scale)
    vec = [done[0][i, :own] for i in range(6)]
    return (
        block_out[None],
        input_grad[None],
        vec[0],
        vec[1],
        done[1],
        done[2],
        done[3],
        done[4],
        vec[2],
        vec[3],
        done[5],
        done[6],
        vec[4],
        vec[5],
        done[7],
        done[8],
    )


def solution(mesh):
    in_specs = (
        P(("fsdp", "rep"), None, None),
        P(("fsdp", "rep"), None, None),
        P(("fsdp", "rep")),
        P(("fsdp", "rep")),
        P("fsdp"),
        P("fsdp"),
        P("fsdp", None),
        P("fsdp", None),
        P("fsdp", None),
        P("fsdp", None),
        P("fsdp"),
        P("fsdp"),
        P("fsdp", None),
        P("fsdp", None),
        P("fsdp"),
        P("fsdp"),
        P("fsdp", None),
        P("fsdp", None),
        P(("fsdp", "rep"), None, None),
    )
    out_specs = (
        P(("fsdp", "rep"), None, None),
        P(("fsdp", "rep"), None, None),
        P("fsdp"),
        P("fsdp"),
        P("fsdp", None),
        P("fsdp", None),
        P("fsdp", None),
        P("fsdp", None),
        P("fsdp"),
        P("fsdp"),
        P("fsdp", None),
        P("fsdp", None),
        P("fsdp"),
        P("fsdp"),
        P("fsdp", None),
        P("fsdp", None),
    )
    return jax.shard_map(shards, mesh=mesh, in_specs=in_specs, out_specs=out_specs, check_vma=False)
```

time: 1490 us -> 534 us (0.36)
  waiting for transfers between devices: 669 us -> 0 us
  Pallas kernels: 0 us -> 337 us
  matrix products: 372 us -> 121 us
  blocking collectives: 158 us -> 0 us
  other arithmetic: 166 us -> 26 us
  local copies, waits for them, and re-layouts: 86.3 us -> 40.1 us
  between operations: 18.4 us -> 3.1 us
    pallas_call x0 -> x6, Pallas kernels: none -> 337 us  [the longest x1 127 us: gather_all(): pl.pallas_call(functools.partial(gather_kernel, dims=dims, pieces=pieces,...]
    reduce_scatter x4 -> x0, waiting for transfers between devices: 300 us -> none  [the longest x1 174 us: shards(): lax.psum_scatter(block_terms[6], 'fsdp', scatter_dimension=0, tiled=True)]
    dot_general x46 -> x26, matrix products: 372 us -> 121 us  [dg(): return lax.dot_general(a, b, dims, preferred_element_type=F32)]
    all_gather x8 -> x0, waiting for transfers between devices: 251 us -> none  [the longest x1 70.8 us: shards(): lax.all_gather(mlp_down, 'fsdp', axis=0, tiled=True)]
    unnamed x2 -> x0, blocking collectives: 156 us -> none
    all_to_all x2 -> x0, waiting for transfers between devices: 113 us -> none  [sum_at_owner(): lax.all_to_all(tiles, axis, split_axis=0, concat_axis=0, tiled=True)]
    convert_element_type x30 -> x2, other arithmetic: 99.6 us -> 1.26 us  [the longest x1 0.77 us: shards(): norms = whole[0][:, :6, :own].transpose(1, 0, 2).reshape(6, D).astype(F32)]
    reduce_sum x15 -> x6, other arithmetic: 53.3 us -> 8.27 us  [the longest x2 6.77 us: norm_back(): return (back, jnp.sum(grad * normal, 0), jnp.sum(grad, 0))]
  transfers between devices with their start and end apart: 15 -> 0, of which waited for: 9 -> 0; matrix products, arithmetic and copies ran while one was open for 34% -> 0% of each run, Pallas kernels for 0% -> 0%
where the time goes in v1:
time: 534 us; the launch traced here: 527 us
  Pallas kernels  337 us (63%)
  matrix products  121 us (23%)
  local copies, waits for them, and re-layouts  40.1 us (8%)
  other arithmetic  26 us (5%)
    pallas_call x1, Pallas kernels, gather_all(): pl.pallas_call(functools.partial(gather_kernel, dims=dims, pieces=pieces,...  127 us
    dot_general x26, matrix products, dg(): return lax.dot_general(a, b, dims, preferred_element_type=F32)  121 us
    pallas_call x1, Pallas kernels, scatter_all(): pl.pallas_call(functools.partial(scatter_kernel, dims=dims, pieces=pieces...  98.6 us
    pallas_call x2, Pallas kernels, attn_bwd(): pl.pallas_call(functools.partial(bwd_kernel, causal=causal, bq=bq, bk=bk,...  66.1 us
    pallas_call x2, Pallas kernels, attn_fwd(): pl.pallas_call(functools.partial(fwd_kernel, causal=causal, bq=bq, unit=u...  45 us
    unnamed x98, local copies, waits for them, and re-layouts  28.3 us

profile of v1, /device:TPU:0, one launch (start us, length us, event | category | flops | bytes accessed | tf_op | source)
XLA Modules:
  0.0 526.9 jit_solution(1383273143002992407)
XLA Ops:
  8.6 127.3 %gather_weights.1 = (bf16[4,2,2,16,256]{4,3,2,1,0:T(8,128)(2,1)}, bf16[4,2,2,48,768]{4,3,2,1,0:T(8,128)(2,1)}, bf16[4,2,2,48,768]{4,3,2,1,0:T(8,128)(2,1)}, bf16...) custom-call(bf16[16,256]{1,0:T(8,128)(2,1)} %pad.8.refs_0_, ...), custom_call_target="tpu_custom_call" | custom-call | tf_op jit(solution)/shard_map/gather_weights/pallas_call | solution.py:314
  137.2 3.5 convolution_convert_fusion.7.q_ref
  144.8 26.8 %attn_fwd.2 = (bf16[1024,768]{1,0:T(8,128)(2,1)S(1)}, f32[6,2,1024]{2,1,0:T(2,128)S(1)}) custom-call(s32[1]{0:T(128)S(6)} %copy.85.n_ref, bf16[1024,768]{1,0:T(8,128)(2,1)S(1)} %convolution_convert_fusion.7.q_ref, bf16[1024,768]{1,0:T(8,128)(2,1)S(1)} %fusion.51.k_ref, bf16[1024,768]{1,0:T(8,128)(2,1)} %fusion.54.v_ref), custom_call_target="tpu_custom_call" | custom-call | tf_op jit(solution)/shard_map/attn_fwd/pallas_call | solution.py:57
  176.3 5.6 %convolution_convert_fusion.q_ref.k_ref.v_ref = bf16[1024,2304]{1,0:T(8,128)(2,1)} fusion(bf16[1024,768]{0,1:T(8,128)(2,1)S(1)} %add_convert_fusion.1, bf16[768,2304]{1,0:T(8,128)(2,1)S(1)} %bitcast.188), kind=kOutput, calls=%fused_computation.11 | convolution fusion | flops 3626237952 | bytes 9830400 | tf_op jit(solution)/shard_map/dot_general | solution.py:19
  181.9 18.2 %attn_fwd.3 = (bf16[1024,768]{1,0:T(8,128)(2,1)S(1)}, f32[6,2,1024]{2,1,0:T(2,128)S(1)}) custom-call(s32[1]{0:T(128)} %copy.84.n_ref, bf16[1024,2304]{1,0:T(8,128)(2,1)} %convolution_convert_fusion.q_ref.k_ref.v_ref, bf16[1024,2304]{1,0:T(8,128)(2,1)} %convolution_convert_fusion.q_ref.k_ref.v_ref, bf16[1024,2304]{1,0:T(8,128)(2,1)} %convolution_convert_fusion.q_ref.k_ref.v_ref), custom_call_target="tpu_custom_call" | custom-call | tf_op jit(solution)/shard_map/attn_fwd/pallas_call | solution.py:57
  200.1 3.3 fusion.73
  203.9 8.3 %fusion.71 = f32[1024,3072]{1,0:T(8,128)} fusion(bf16[768,3072]{1,0:T(8,128)(2,1)S(1)} %bitcast.174, f32[1024,768]{0,1:T(8,128)S(1)} %get-tuple-element.117, f32[768]{0:T(1024)S(1)} %add.109, f32[768]{0:T(1024)S(1)} %mul.216, f32[1024]{0:T(1024)S(1)} %add_rsqrt_fusion, f32[1024]{0:T(1024)S(1)} %broadcast_multiply_fusion.6), kind=kOutput, calls=%fused_computation.136 | convolution fusion | flops 4835770368 | bytes 20461568 | tf_op jit(solution)/shard_map/dot_general | solution.py:19
  212.2 11.0 %fusion.50 = bf16[1,1024,768]{1,2,0:T(8,128)(2,1)} fusion(f32[1024,768]{0,1:T(8,128)S(1)} %get-tuple-element.117, bf16[3072,768]{1,0:T(8,128)(2,1)} %bitcast.200, pred[1024]{0:T(1024)(128)(4,1)S(1)} %iota_compare_fusion, f32[1024,3072]{1,0:T(8,128)} %fusion.71), kind=kOutput, calls=%fused_computation.89 | convolution fusion | flops 4862509056 | bytes 22021120 | tf_op jit(solution)/shard_map/dot_general | solution.py:19
  225.8 18.5 %fusion.7 = bf16[1024,3072]{1,0:T(8,128)(2,1)S(1)} fusion(f32[1024,3072]{1,0:T(8,128)} %fusion.71, bf16[3072,768]{1,0:T(8,128)(2,1)} %bitcast.201, bf16[1,1024,768]{1,2,0:T(8,128)(2,1)} %copy.53, pred[1024]{0:T(1024)(128)(4,1)S(1)} %iota_compare_fusion), kind=kOutput, calls=%fused_computation.9 | convolution fusion | flops 4893966336 | bytes 25166848 | tf_op jit(solution)/shard_map/dot_general | solution.py:19
  244.3 13.0 %convolution_convert_fusion.2 = bf16[3072,768]{1,0:T(8,128)(2,1)} fusion(bf16[1,1024,768]{1,2,0:T(8,128)(2,1)S(1)} %copy-done.18, pred[1024]{0:T(1024)(128)(4,1)S(1)} %iota_compare_fusion, f32[1024,3072]{1,0:T(8,128)} %fusion.71), kind=kOutput, calls=%fused_computation.13 | convolution fusion | flops 4864868352 | bytes 18875392 | tf_op jit(solution)/shard_map/dot_general | solution.py:19
  257.3 9.3 %fusion.75 = (bf16[768]{0:T(1024)(128)(2,1)S(1)}, f32[1024,768]{1,0:T(8,128)}) fusion(bf16[1024,3072]{1,0:T(8,128)(2,1)S(1)} %fusion.7, bf16[768,3072]{1,0:T(8,128)(2,1)} %bitcast.171), kind=kOutput, calls=%fused_computation.140 | convolution fusion | flops 4832623616 | bytes 14157312 | tf_op jit(solution)/shard_map/dot_general | solution.py:19
  266.6 7.0 %convolution_convert_fusion.1 = bf16[768,3072]{1,0:T(8,128)(2,1)} fusion(bf16[1024,3072]{1,0:T(8,128)(2,1)S(1)} %fusion.7, f32[1024,768]{0,1:T(8,128)S(1)} %copy-done.9, f32[768]{0:T(1024)S(1)} %add.109, f32[768]{0:T(1024)S(1)} %mul.216, f32[1024]{0:T(1024)S(1)} %add_rsqrt_fusion, f32[1024]{0:T(1024)S(1)} %broadcast_multiply_fusion.6), kind=kOutput, calls=%fused_computation.12 | convolution fusion | flops 4838129664 | bytes 14170112 | tf_op jit(solution)/shard_map/dot_general | solution.py:19
  273.7 3.5 copy.54
  277.2 3.8 multiply_reduce_fusion
  281.1 4.5 fusion.24
  288.2 29.3 %attn_bwd.2 = bf16[3,1024,768]{2,1,0:T(8,128)(2,1)} custom-call(s32[1]{0:T(128)} %copy.84.n_ref, bf16[1024,2304]{1,0:T(8,128)(2,1)} %convolution_convert_fusion.q_ref.k_ref.v_ref, bf16[1024,2304]{1,0:T(8,128)(2,1)} %convolution_convert_fusion.q_ref.k_ref.v_ref, bf16[1024,2304]{1,0:T(8,128)(2,1)} %convolution_convert_fusion.q_ref.k_ref.v_ref, ...), custom_call_target="tpu_custom_call" | custom-call | tf_op jit(solution)/shard_map/attn_bwd/pallas_call | solution.py:112
  331.4 3.8 multiply_reduce_fusion.1
  335.3 6.3 %multiply_add_fusion.1 = f32[1024,768]{0,1:T(8,128)} fusion(f32[1024,768]{0,1:T(8,128)} %copy-done.16, f32[1024,768]{0,1:T(8,128)} %get-tuple-element.118, f32[1024,768]{0,1:T(8,128)} %copy-done.10, f32[1024]{0:T(1024)S(1)} %broadcast_multiply_fusion.2, f32[1024]{0:T(1024)S(1)} %broadcast_multiply_fusion.3, f32[768]{0:T(1024)S(1)} %mul.210, ...), kind=kLoop, calls=%fused_computation.43 | loop fusion | flops 6291456 | bytes 12602368 | tf_op jit(solution)/shard_map/add | solution.py:584
  341.7 5.0 convolution_convert_fusion.5.do_ref
  346.7 36.8 %attn_bwd.3 = bf16[3,1024,768]{2,1,0:T(8,128)(2,1)} custom-call(s32[1]{0:T(128)S(6)} %copy.85.n_ref, bf16[1024,768]{1,0:T(8,128)(2,1)S(1)} %convolution_convert_fusion.7.q_ref, bf16[1024,768]{1,0:T(8,128)(2,1)S(1)} %copy-done.2, bf16[1024,768]{1,0:T(8,128)(2,1)S(1)} %copy-done.3, bf16[1024,768]{1,0:T(8,128)(2,1)} %copy-done.6, ...), custom_call_target="tpu_custom_call" | custom-call | tf_op jit(solution)/shard_map/attn_bwd/pallas_call | solution.py:112
  397.5 3.6 copy.58
  404.1 5.6 %fusion.19 = f32[1,1024,768]{1,2,0:T(8,128)} fusion(f32[1024,768]{0,1:T(8,128)} %multiply_add_fusion.1, bf16[1,1024,768]{1,2,0:T(8,128)(2,1)S(1)} %copy-done.14, f32[1024,768]{0,1:T(8,128)} %copy.58, f32[1024]{0:T(1024)S(1)} %broadcast_multiply_fusion, f32[1024]{0:T(1024)S(1)} %broadcast_multiply_fusion.1, f32[768]{0:T(1024)S(1)} %copy-done.29, ...), kind=kLoop, calls=%fused_computation.30 | loop fusion | flops 7077888 | bytes 11029504 | tf_op jit(solution)/shard_map/broadcast_in_dim | solution.py:617
  409.7 3.5 copy.63
  414.0 98.6 %scatter_grads.1 = (f32[16,256]{1,0:T(8,128)}, f32[48,768]{1,0:T(8,128)}, f32[48,768]{1,0:T(8,128)}, f32[48,768]{1,0:T(8,128)}, f32[48,768]{1,0:T(8,128)}, /*ind...) custom-call(bf16[4,2,2,192,768]{4,3,2,1,0:T(8,128)(2,1)} %bitcast.175, ...), custom_call_target="tpu_custom_call" | custom-call | tf_op jit(solution)/shard_map/scatter_grads/pallas_call | solution.py:462
  (150 shorter events, 67.7 us)
Async XLA Ops:
  0.6 140.2 %copy-start = (bf16[1,1024,768]{2,1,0:T(8,128)(2,1)S(1)}, bf16[1,1024,768]{2,1,0:T(8,128)(2,1)}, u32[]{:S(2)}) copy-start(bf16[1,1024,768]{2,1,0:T(8,128)(2,1)} %param.20) | copy-start | bytes 4718596
  5.2 3.4 copy-start.12
  5.5 135.3 %copy-start.26 = (f32[1024]{0:T(1024)}, f32[1024]{0:T(1024)S(1)}, u32[]{:S(2)}) copy-start(f32[1024]{0:T(1024)S(1)} %broadcast_multiply_fusion.8) | copy-start | bytes 12292
  5.9 134.8 %copy-start.30 = (f32[1024]{0:T(1024)}, f32[1024]{0:T(1024)S(1)}, u32[]{:S(2)}) copy-start(f32[1024]{0:T(1024)S(1)} %add_rsqrt_fusion.2) | copy-start | bytes 12292
  136.9 3.9 copy-start.28
  137.1 3.7 copy-start.32
  137.2 3.6 copy-start.37
  144.8 26.8 %copy-start.13 = (bf16[1,1024,768]{1,2,0:T(8,128)(2,1)S(1)}, bf16[1,1024,768]{1,2,0:T(8,128)(2,1)}, u32[]{:S(2)}) copy-start(bf16[1,1024,768]{1,2,0:T(8,128)(2,1)} %copy-done.12) | copy-start | bytes 4718596
  144.8 26.9 %copy-start.35 = (bf16[4,2,2,48,768]{4,3,2,1,0:T(8,128)(2,1)S(1)}, bf16[4,2,2,48,768]{4,3,2,1,0:T(8,128)(2,1)}, u32[]{:S(2)}) copy-start(bf16[4,2,2,48,768]{4,3,2,1,0:T(8,128)(2,1)} %get-tuple-element.43) | copy-start | bytes 3538948
  173.2 27.0 %copy-start.10 = (f32[1024,768]{0,1:T(8,128)}, f32[1024,768]{0,1:T(8,128)S(1)}, u32[]{:S(2)}) copy-start(f32[1024,768]{0,1:T(8,128)S(1)} %get-tuple-element.115) | copy-start | bytes 9437188
  176.3 5.6 %copy-start.20 = (bf16[1024,768]{0,1:T(8,128)(2,1)}, bf16[1024,768]{0,1:T(8,128)(2,1)S(1)}, u32[]{:S(2)}) copy-start(bf16[1024,768]{0,1:T(8,128)(2,1)S(1)} %add_convert_fusion.1) | copy-start | bytes 4718596
  200.1 3.4 copy-start.4
  200.1 3.8 slice-start
  200.1 3.8 slice-start.1
  203.5 8.8 %copy-start.8 = (f32[1024,768]{0,1:T(8,128)}, f32[1024,768]{0,1:T(8,128)S(1)}, u32[]{:S(2)}) copy-start(f32[1024,768]{0,1:T(8,128)S(1)} %get-tuple-element.117) | copy-start | bytes 9437188
  225.8 18.5 %copy-start.18 = (bf16[1,1024,768]{1,2,0:T(8,128)(2,1)S(1)}, bf16[1,1024,768]{1,2,0:T(8,128)(2,1)}, u32[]{:S(2)}) copy-start(bf16[1,1024,768]{1,2,0:T(8,128)(2,1)} %copy.53) | copy-start | bytes 4718596
  257.3 9.3 %copy-start.9 = (f32[1024,768]{0,1:T(8,128)S(1)}, f32[1024,768]{0,1:T(8,128)}, u32[]{:S(2)}) copy-start(f32[1024,768]{0,1:T(8,128)} %copy-done.8) | copy-start | bytes 9437188
  281.1 4.5 copy-start.22
  285.6 31.9 %copy-start.16 = (f32[1024,768]{0,1:T(8,128)}, f32[1024,768]{0,1:T(8,128)S(1)}, u32[]{:S(2)}) copy-start(f32[1024,768]{0,1:T(8,128)S(1)} %fusion.24) | copy-start | bytes 9437188
  341.7 5.0 copy-start.2
  341.7 5.0 copy-start.3
  346.7 36.8 %copy-start.7 = (bf16[1024,768]{1,0:T(8,128)(2,1)S(1)}, bf16[1024,768]{1,0:T(8,128)(2,1)}, u32[]{:S(2)}) copy-start(bf16[1024,768]{1,0:T(8,128)(2,1)} %copy-done.6) | copy-start | bytes 4718596
  346.7 36.8 %copy-start.15 = (f32[1024,768]{0,1:T(8,128)S(1)}, f32[1024,768]{0,1:T(8,128)}, u32[]{:S(2)}) copy-start(f32[1024,768]{0,1:T(8,128)} %multiply_add_fusion.1) | copy-start | bytes 9437188
  512.6 13.1 %copy-start.23 = (f32[192,768]{1,0:T(8,128)S(1)}, f32[192,768]{1,0:T(8,128)}, u32[]{:S(2)}) copy-start(f32[192,768]{1,0:T(8,128)} %get-tuple-element.156) | copy-start | bytes 1769476
  (16 other events, 41.9 us)

commit v2 on v1

v2 whole, which is shorter than its diff:
```python
import functools

import jax
import jax.numpy as jnp
from jax import lax
from jax.experimental import pallas as pl
from jax.experimental.pallas import tpu as pltpu
from jax.sharding import PartitionSpec as P

D = 768
FRAME_TOK = 256
EPS = 1e-05
MESH = pl.DeviceIdType.MESH
VMEM_BYTES = 58 << 20

F32, BF16 = jnp.float32, jnp.bfloat16
NN = (((1,), (0,)), ((), ()))
NT = (((1,), (1,)), ((), ()))
TN = (((0,), (0,)), ((), ()))
def dg(a, b, dims): return lax.dot_general(a, b, dims, preferred_element_type=F32)

def head_sides(side, q2, k2, bias):
    lane = lax.broadcasted_iota(jnp.int32, (1, 128), 1)
    mine = (lane >= 64) if side else (lane < 64)
    extra = lane == (0 if side else 64)
    qa = jnp.where(mine, q2, jnp.where(extra, 1.0, 0.0).astype(BF16))
    ka = jnp.where(mine, k2, jnp.where(extra, bias, 0.0).astype(BF16))
    return qa, ka

def fwd_kernel(n_ref, q_ref, k_ref, v_ref, o_ref, l_ref, vt, *, causal, bq, unit, at):
    T = q_ref.shape[0]; K = k_ref.shape[0]
    live = n_ref[0] * unit
    bias = jnp.where(lax.broadcasted_iota(jnp.int32, (K, 1), 0) < live, 0.0, -1e30).astype(F32)
    q2 = q_ref[...] * BF16(0.125)
    k2 = k_ref[...]
    vt[...] = v_ref[...].T
    for side in range(2):
        at(side)
        qa, ka = head_sides(side, q2, k2, bias)
        for j in range(T // bq):
            span = (j + 1) * bq if causal else K
            s = dg(ka[:span], qa[j * bq:(j + 1) * bq], NT)
            if causal:
                top = j * bq
                diag = s[top:]
                ok = lax.broadcasted_iota(jnp.int32, (bq, bq), 0) <= lax.broadcasted_iota(jnp.int32, (bq, bq), 1)
                diag = jnp.where(ok, diag, -1e30)
                s = diag if top == 0 else jnp.concatenate([s[:top], diag], 0)
            m = jnp.max(s, 0, keepdims=True)
            p = jnp.exp(s - m)
            l = jnp.sum(p, 0, keepdims=True)
            ot = dg(vt[side * 64:(side + 1) * 64, :span], p.astype(BF16), NN) * (1.0 / l)
            o_ref[j * bq:(j + 1) * bq, side * 64:(side + 1) * 64] = ot.T.astype(BF16)
            l_ref[0, side:side + 1, j * bq:(j + 1) * bq] = m + jnp.log(l)


def bwd_kernel(n_ref, q_ref, k_ref, v_ref, o_ref, do_ref, l_ref, g_ref, kt, dqt, dka, dva, *, causal, bq, bk, unit, at):
    T = q_ref.shape[0]; K = k_ref.shape[0]
    live = n_ref[0] * unit
    bias = jnp.where(lax.broadcasted_iota(jnp.int32, (K, 1), 0) < live, 0.0, -1e30).astype(F32)
    q2 = q_ref[...] * BF16(0.125)
    k2 = k_ref[...]; v2 = v_ref[...]
    do2 = do_ref[...]
    kt[...] = k2.T
    prod = (do2.astype(F32) * o_ref[...].astype(F32)).T
    lane = lax.broadcasted_iota(jnp.int32, (1, 128), 1)
    for side in range(2):
        at(side)
        qa, ka = head_sides(side, q2, k2, bias)
        mine = (lane >= 64) if side else (lane < 64)
        va = jnp.where(mine, v2, BF16(0))
        delta = jnp.sum(prod[side * 64:(side + 1) * 64], 0, keepdims=True)
        lse = l_ref[0, side:side + 1, :]
        for i in range(K // bk):
            dk = dv = None
            kb, vb = ka[i * bk:(i + 1) * bk], va[i * bk:(i + 1) * bk]
            for j in range(T // bq):
                if causal and (j + 1) * bq <= i * bk: continue
                cols = slice(j * bq, (j + 1) * bq)
                s = dg(kb, qa[cols], NT)
                p = jnp.exp(s - lse[:, cols])
                if causal and j * bq < (i + 1) * bk:
                    ok = i * bk + lax.broadcasted_iota(jnp.int32, (bk, bq), 0) <= j * bq + lax.broadcasted_iota(jnp.int32, (bk, bq), 1)
                    p = jnp.where(ok, p, 0.0)
                dp = dg(vb, do2[cols], NT)
                ds = (p * (dp - delta[:, cols])).astype(BF16)
                a = dg(p.astype(BF16), do2[cols], NN)
                b = dg(ds, q2[cols], NN)
                dv = a if dv is None else dv + a
                dk = b if dk is None else dk + b
                c = dg(kt[side * 64:(side + 1) * 64, i * bk:(i + 1) * bk], ds, NN)
                if i == 0: dqt[side * 64:(side + 1) * 64, cols] = c
                else: dqt[side * 64:(side + 1) * 64, cols] += c
            rows = slice(i * bk, (i + 1) * bk)
            if side == 0:
                dka[rows] = dk; dva[rows] = dv
            else:
                g_ref[1, rows, :] = jnp.where(lane < 64, dka[rows], dk).astype(BF16)
                g_ref[2, rows, :] = jnp.where(lane < 64, dva[rows], dv).astype(BF16)
    g_ref[0] = (dqt[...] * 0.125).T.astype(BF16)


def grid_of(n):
    if n == 16:
        return 4, 2, 2
    if n == 64:
        return 4, 4, 4
    return n, 1, 1


def cut(shapes):
    out = []
    for i, (rows, cols) in enumerate(shapes):
        step = 256 if rows > cols // 8 and cols == 768 else min(cols, 768)
        out += [(i, c, step) for c in range(0, cols, step)]
    return out


def remote(src, dst, send, recv, dev):
    return pltpu.make_async_remote_copy(
        src_ref=src, dst_ref=dst, send_sem=send, recv_sem=recv, device_id=dev, device_id_type=MESH
    )


class Place:
    def __init__(self, dims):
        self.dims = dims
        self.size = dict(zip("zyx", dims))
        Z, Y, X = dims
        self.me = lax.axis_index("fsdp")
        self.core = lax.axis_index("rep")
        self.mine = {"z": self.me // (Y * X), "y": (self.me // X) % Y, "x": self.me % X}

    def peers(self, axis):
        mine, count = self.mine[axis], self.size[axis]
        out = []
        for k in range(1, count):
            at = dict(self.mine)
            at[axis] = (mine + k) % count
            dev = ((at["z"] * self.size["y"] + at["y"]) * self.size["x"] + at["x"], self.core)
            out.append((at[axis], (mine + count - k) % count, dev))
        return out

    def sibling(self):
        return (self.me, 1 - self.core)

    def greet(self):
        bar = pltpu.get_barrier_semaphore()
        devs = [d for axis in "zyx" for _, _, d in self.peers(axis)] + [self.sibling()]
        for d in devs:
            pl.semaphore_signal(bar, inc=1, device_id=d, device_id_type=MESH)
        pl.semaphore_wait(bar, len(devs))

    def by_core(self, action):
        @pl.when(self.core == 0)
        def _():
            action(0, "x", "y")

        @pl.when(self.core == 1)
        def _():
            action(1, "y", "x")


class Gather:
    def __init__(self, shapes, n):
        self.dims = grid_of(n)
        self.pieces = cut(shapes)
        self.count = len(shapes)
        self.shapes = shapes
        self.steps = len(self.pieces) + 2

    def outs(self):
        return [jax.ShapeDtypeStruct(self.dims + tuple(s), BF16) for s in self.shapes]

    def scratch(self):
        Z, Y, X = self.dims
        M, z, s = len(self.pieces), max(self.dims[0] - 1, 1), max(Y - 1, X - 1, 1)
        sem = pltpu.SemaphoreType.DMA
        return [sem((self.count,))] + [sem((M, c)) for c in (z, z, s, s, s, s, z, z, s, s, s, s)]

    def bind(self, shards, outs, scratch):
        self.shards, self.out = shards, outs
        self.own, *self.sem = scratch
        self.place = Place(self.dims)

    def half(self, m, side):
        _, c, w = self.pieces[m]
        return pl.ds(c + side * (w // 2), w // 2)

    def view(self, m, side, at):
        z, y, x = [slice(None) if at.get(k) is None else at[k] for k in "zyx"]
        return self.out[self.pieces[m][0]].at[z, y, x, :, self.half(m, side)]

    def hop(self, stage, m, side, axes, coming):
        a, b = axes
        mine = self.place.mine
        axis = ("z", a, b)[stage]
        out = []
        for k, (_, frm, dev) in enumerate(self.place.peers(axis)):
            at = dict(mine)
            for done in ("z", a)[:stage]:
                at[done] = None
            if coming:
                at[axis] = frm
            v = self.view(m, side, at)
            src = v
            if stage == 0 and not coming:
                src = self.shards[self.pieces[m][0]].at[:, self.half(m, side)]
            s, r = self.sem[2 * stage : 2 * stage + 2]
            out.append((at, lambda v=v, src=src, s=s, r=r, k=k, dev=dev: remote(src, v, s.at[m, k], r.at[m, k], dev)))
        return out

    def give(self, stage, m, side, at, k):
        v = self.view(m, side, at)
        s, r = self.sem[6 + 2 * stage : 8 + 2 * stage]
        return remote(v, v, s.at[m, k], r.at[m, k], self.place.sibling())

    def own_copies(self):
        p = self.place.mine
        return [
            pltpu.make_async_copy(s, o.at[p["z"], p["y"], p["x"]], self.own.at[i])
            for i, (s, o) in enumerate(zip(self.shards, self.out))
        ]

    def begin(self):
        for c in self.own_copies():
            c.start()

        def go(core, a, b):
            for m in range(len(self.pieces)):
                for _, c in self.hop(0, m, core, (a, b), False):
                    c().start()

        self.place.by_core(go)

    def step(self, t):
        if t == 0:
            for c in self.own_copies():
                c.wait()

        def go(core, a, b):
            for stage in range(3):
                m = t - stage
                if not 0 <= m < len(self.pieces):
                    continue
                came = self.hop(stage, m, core, (a, b), True)
                for _, c in came:
                    c().wait_recv()
                if stage < 2:
                    for _, c in self.hop(stage + 1, m, core, (a, b), False):
                        c().start()
                for k, (at, _) in enumerate(came):
                    self.give(stage, m, core, at, k).start()

        self.place.by_core(go)

    def end(self):
        def go(core, a, b):
            for m in range(len(self.pieces)):
                for stage in range(3):
                    for k, (at, c) in enumerate(self.hop(stage, m, core, (a, b), False)):
                        c().wait_send()
                    for k, (at, _) in enumerate(self.hop(stage, m, core, (a, b), True)):
                        self.give(stage, m, core, at, k).wait_send()
                    for k, (at, _) in enumerate(self.hop(stage, m, core, (b, a), True)):
                        self.give(stage, m, 1 - core, at, k).wait_recv()

        self.place.by_core(go)


class Scatter:
    def __init__(self, shapes, targets, n):
        self.dims = grid_of(n)
        self.pieces = [(i, c, w, targets[i][0], targets[i][1] + c) for i, c, w in cut(shapes)]
        self.shapes, self.targets = shapes, targets
        self.steps = len(self.pieces) + 3

    def outs(self):
        width, rows = {}, {}
        for (r, w), (o, c) in zip(self.shapes, self.targets):
            width[o], rows[o] = max(width.get(o, 0), c + w), r
        return [jax.ShapeDtypeStruct((rows[o], width[o]), F32) for o in range(len(width))]

    def scratch(self):
        Z, Y, X = self.dims
        M, S = len(self.pieces), max(Y, X)
        one, z = max(S - 1, 1), max(Z - 1, 1)
        shape = [(self.shapes[i][0], w // 2) for i, _, w, _, _ in self.pieces]
        sem = pltpu.SemaphoreType.DMA
        lead = [(S, S, Z), (S, S, Z), (one, S, Z), (one, Z), (z,)]
        return (
            [[pltpu.VMEM(l + s, BF16) for s in shape] for l in lead]
            + [[pltpu.VMEM((2,) + s, F32) for s in shape]]
            + [sem((M, S * S))] * 3
            + [sem((M, one))] * 4
            + [sem((M, z))] * 2
            + [sem((M,))] * 2
        )

    def bind(self, grads, outs, scratch):
        self.grads, self.out = grads, outs
        self.acc, self.sib, self.got1, self.got2, self.got3, self.fin, self.lsem, *self.sem = scratch
        self.place = Place(self.dims)

    def meet(self, m, core):
        Z, Y, X = self.dims
        i, c, w, _, _ = self.pieces[m]
        for y in range(Y):
            for x in range(X):
                k = y * X + x
                take = [self.grads[i].at[:, y, x, :, pl.ds(c + s * (w // 2), w // 2)] for s in range(2)]
                at = [(y, x), (x, y)]
                yield pltpu.make_async_copy(take[core], self.acc[m].at[at[core]], self.lsem.at[m, k])
                yield remote(
                    take[1 - core],
                    self.sib[m].at[at[1 - core]],
                    self.sem[0].at[m, k],
                    self.sem[1].at[m, k],
                    self.place.sibling(),
                )

    def hop(self, stage, m, axes):
        a, b = axes
        mine = self.place.mine
        s, r = self.sem[2 * stage : 2 * stage + 2]
        got = (None, self.got1, self.got2, self.got3)[stage]
        for k, (there, _, dev) in enumerate(self.place.peers((None, b, a, "z")[stage])):
            at = (mine[b], mine[a])[: stage - 1] + (there,)
            yield remote(self.acc[m].at[at], got[m].at[k], s.at[m, k], r.at[m, k], dev)

    def swap(self, m, side):
        v = self.fin[m].at[side]
        return remote(v, v, self.sem[8].at[m], self.sem[9].at[m], self.place.sibling())

    def add(self, dst, srcs):
        total = dst[...].astype(F32)
        for s in srcs:
            total = total + s[...].astype(F32)
        dst[...] = total.astype(BF16)

    def begin(self):
        def go(core, a, b):
            for m in range(len(self.pieces)):
                for c in self.meet(m, core):
                    c.start()

        self.place.by_core(go)

    def step(self, t):
        def go(core, a, b):
            mine, size = self.place.mine, self.place.size
            for stage in range(4):
                m = t - stage
                if not 0 <= m < len(self.pieces):
                    continue
                acc = self.acc[m]
                if stage == 0:
                    for c in self.meet(m, core):
                        c.wait()
                    for j in range(size[b]):
                        self.add(acc.at[j, : size[a]], [self.sib[m].at[j, : size[a]]])
                else:
                    for c in self.hop(stage, m, (a, b)):
                        c.wait_recv()
                if stage == 1:
                    self.add(
                        acc.at[mine[b], : size[a]],
                        [self.got1[m].at[k, : size[a]] for k in range(size[b] - 1)],
                    )
                if stage == 2:
                    self.add(
                        acc.at[mine[b], mine[a]], [self.got2[m].at[k] for k in range(size[a] - 1)]
                    )
                if stage == 3:
                    total = acc[mine[b], mine[a], mine["z"]].astype(F32)
                    for k in range(size["z"] - 1):
                        total = total + self.got3[m][k].astype(F32)
                    self.fin[m][core] = total
                    self.swap(m, core).start()
                else:
                    for c in self.hop(stage + 1, m, (a, b)):
                        c.start()

        self.place.by_core(go)

    def end(self):
        def go(core, a, b):
            for m in range(len(self.pieces)):
                for stage in range(1, 4):
                    for c in self.hop(stage, m, (a, b)):
                        c.wait_send()
                self.swap(m, core).wait_send()
                self.swap(m, 1 - core).wait_recv()

        self.place.by_core(go)
        for m, (i, c, w, o, at) in enumerate(self.pieces):
            for side in range(2):
                self.out[o][:, at + side * (w // 2) : at + (side + 1) * (w // 2)] = self.fin[m][side]


def alone(engine, operands, cid, name):
    def kernel(*refs):
        count, outs = len(operands), len(engine.outs())
        engine.bind(refs[:count], refs[count : count + outs], refs[count + outs :])
        engine.place.greet()
        engine.begin()
        for t in range(engine.steps):
            engine.step(t)
        engine.end()

    space = pl.ANY if isinstance(engine, Gather) else pltpu.VMEM
    return pl.pallas_call(
        kernel,
        out_shape=engine.outs(),
        in_specs=[pl.BlockSpec(memory_space=pl.ANY)] * len(operands),
        out_specs=[pl.BlockSpec(memory_space=space)] * len(engine.outs()),
        scratch_shapes=engine.scratch(),
        compiler_params=pltpu.CompilerParams(
            collective_id=cid, has_side_effects=True, vmem_limit_bytes=VMEM_BYTES
        ),
        name=name,
    )(*operands)


class Beside:
    def __init__(self, engine, points):
        self.engine = engine
        self.points = points

    def reach(self, i, side):
        e = self.engine
        if side == 0:

            @pl.when(i == 0)
            def _():
                e.place.greet()
                e.begin()

        for t, p in enumerate(self.points):
            if p is not None and p % 2 == side:

                @pl.when(i == p // 2)
                def _(t=t):
                    e.step(t)

    def close(self, i):
        e = self.engine

        @pl.when(i == pl.num_programs(0) - 1)
        def _():
            for t, p in enumerate(self.points):
                if p is None:
                    e.step(t)
            e.end()


def paced(engine, first, each, unit, units=12):
    points = []
    for t in range(engine.steps):
        p = int(-(-(first + t * each) // unit))
        points.append(p if p < units else None)
    return points


def attend_beside(body, attn_in, in_specs, attn_out, out_specs, attn_scratch, engine, operands, points, cid, name):
    nin, nout, nscr = len(attn_in), len(attn_out), len(attn_scratch)
    moved, landed = len(operands), len(engine.outs())

    def kernel(*refs):
        at = 0
        groups = []
        for count in (nin, moved, nout, landed, nscr):
            groups.append(refs[at : at + count])
            at += count
        engine.bind(groups[1], groups[3], refs[at:])
        beside = Beside(engine, points)
        i = pl.program_id(0)
        body(*groups[0], *groups[2], *groups[4], at=lambda side: beside.reach(i, side))
        beside.close(i)

    any_ = pl.BlockSpec(memory_space=pl.ANY)
    space = pl.ANY if isinstance(engine, Gather) else pltpu.VMEM
    outs = pl.pallas_call(
        kernel,
        grid=(6,),
        in_specs=in_specs + [any_] * moved,
        out_specs=out_specs + [pl.BlockSpec(memory_space=space)] * landed,
        out_shape=attn_out + engine.outs(),
        scratch_shapes=attn_scratch + engine.scratch(),
        compiler_params=pltpu.CompilerParams(
            collective_id=cid, has_side_effects=True, vmem_limit_bytes=VMEM_BYTES
        ),
        name=name,
    )(*attn_in, *operands)
    return outs[:nout], outs[nout:]


def attn_fwd(live, q, k, v, cols, causal, unit, bq, engine, operands, points, cid, name):
    T, K = q.shape[0], k.shape[0]
    qo, ko, vo = cols
    return attend_beside(
        functools.partial(fwd_kernel, causal=causal, bq=bq, unit=unit),
        [live, q, k, v],
        [
            pl.BlockSpec(memory_space=pltpu.SMEM),
            pl.BlockSpec((T, 128), lambda i: (0, i + qo)),
            pl.BlockSpec((K, 128), lambda i: (0, i + ko)),
            pl.BlockSpec((K, 128), lambda i: (0, i + vo)),
        ],
        [jax.ShapeDtypeStruct((T, D), BF16), jax.ShapeDtypeStruct((6, 2, T), F32)],
        [pl.BlockSpec((T, 128), lambda i: (0, i)), pl.BlockSpec((1, 2, T), lambda i: (i, 0, 0))],
        [pltpu.VMEM((128, K), BF16)],
        engine,
        operands,
        points,
        cid,
        name,
    )


def attn_bwd(live, q, k, v, o, do, lse, cols, causal, unit, bq, bk, engine, operands, points, cid, name):
    T, K = q.shape[0], k.shape[0]
    qo, ko, vo = cols
    return attend_beside(
        functools.partial(bwd_kernel, causal=causal, bq=bq, bk=bk, unit=unit),
        [live, q, k, v, o, do, lse],
        [
            pl.BlockSpec(memory_space=pltpu.SMEM),
            pl.BlockSpec((T, 128), lambda i: (0, i + qo)),
            pl.BlockSpec((K, 128), lambda i: (0, i + ko)),
            pl.BlockSpec((K, 128), lambda i: (0, i + vo)),
            pl.BlockSpec((T, 128), lambda i: (0, i)),
            pl.BlockSpec((T, 128), lambda i: (0, i)),
            pl.BlockSpec((1, 2, T), lambda i: (i, 0, 0)),
        ],
        [jax.ShapeDtypeStruct((3, T, D), BF16)],
        [pl.BlockSpec((3, T, 128), lambda i: (0, 0, i))],
        [
            pltpu.VMEM((128, K), BF16),
            pltpu.VMEM((128, T), F32),
            pltpu.VMEM((K, 128), F32),
            pltpu.VMEM((K, 128), F32),
        ],
        engine,
        operands,
        points,
        cid,
        name,
    )


def finish(sums, scale):
    def kernel(*refs):
        for i, o in zip(refs[: len(sums)], refs[len(sums) :]):
            o[...] = i[...] * scale

    return pl.pallas_call(
        kernel, out_shape=[jax.ShapeDtypeStruct(s.shape, F32) for s in sums], name="finish"
    )(*sums)


def moments(values):
    average = jnp.mean(values, -1, keepdims=True)
    centred = values - average
    variance = jnp.mean(centred * centred, -1, keepdims=True)
    inverse = lax.rsqrt(variance + EPS)
    return centred * inverse, inverse


def norm_back(normal, inverse, gain, grad):
    m = grad * gain
    back = inverse * (
        m - jnp.mean(m, -1, keepdims=True) - normal * jnp.mean(m * normal, -1, keepdims=True)
    )
    return back, jnp.sum(grad * normal, 0), jnp.sum(grad, 0)


GELU_A = 0.7978845608028654
GELU_B = 0.044715


def gelu(u):
    return 0.5 * u * (1.0 + jnp.tanh(GELU_A * (u + GELU_B * u * u * u)))


def gelu_slope(u):
    t = jnp.tanh(GELU_A * (u + GELU_B * u * u * u))
    return 0.5 * (1.0 + t) + 0.5 * u * (1.0 - t * t) * (GELU_A * (1.0 + 3.0 * GELU_B * u * u))


def shards(
    tokens,
    context,
    clip_lengths,
    context_frames,
    norm1_gain,
    norm1_bias,
    cross_q,
    cross_k,
    cross_v,
    cross_out,
    norm2_gain,
    norm2_bias,
    attn_qkv,
    attn_out,
    norm3_gain,
    norm3_bias,
    mlp_up,
    mlp_down,
    cotangent,
):
    n = lax.axis_size("fsdp")
    stream_in = tokens[0].astype(F32)
    context_rows = context[0]
    slot_rows = stream_in.shape[0]
    own = norm1_gain.shape[0]
    padding = (jnp.arange(slot_rows) < clip_lengths[0])[:, None]
    norms = jnp.stack([norm1_gain, norm1_bias, norm2_gain, norm2_bias, norm3_gain, norm3_bias])
    norms = jnp.pad(norms, ((0, 10), (0, 256 - own)))

    def flat(arrays):
        return [a.reshape(-1, a.shape[4]) for a in arrays]

    def gather(arrays):
        return Gather([a.shape for a in arrays], n), arrays

    def weight(left, right):
        g = dg(left, right, TN).astype(BF16)
        return g.reshape(n, -1, g.shape[1])

    def scatter(grads):
        arrays = [g.reshape(grid_of(n) + g.shape[1:]) for g, _ in grads]
        return Scatter([a.shape[3:] for a in arrays], [t for _, t in grads], n), arrays

    first, operands = gather([norms, cross_q, cross_k, cross_v])
    norms, *whole = alone(first, operands, 0, "gather_cross")
    w_q, w_k, w_v = flat(whole)
    norms = norms.reshape((n,) + norms.shape[3:])[:, :6, :own].transpose(1, 0, 2).reshape(6, D).astype(F32)
    gain_one, bias_one, gain_two, bias_two, gain_three, bias_three = [norms[i] for i in range(6)]

    normal_one, inverse_one = moments(stream_in)
    h1 = (normal_one * gain_one + bias_one).astype(BF16)
    q1 = dg(h1, w_q, NN).astype(BF16)
    k1 = dg(context_rows, w_k, NN).astype(BF16)
    v1 = dg(context_rows, w_v, NN).astype(BF16)
    second, operands = gather([cross_out, attn_qkv, attn_out])
    (o1, lse1), whole = attn_fwd(
        context_frames, q1, k1, v1, (0, 0, 0), False, FRAME_TOK, 512,
        second, operands, paced(second, 8.0, 4.8, 2.2), 1, "cross_fwd",
    )
    w_o, w_qkv, w_p = flat(whole)
    x1 = stream_in + dg(o1, w_o, NN)
    normal_two, inverse_two = moments(x1)
    h2 = (normal_two * gain_two + bias_two).astype(BF16)
    qkv = dg(h2, w_qkv, NN).astype(BF16)
    third, operands = gather([mlp_up, mlp_down])
    (o2, lse2), whole = attn_fwd(
        clip_lengths, qkv, qkv, qkv, (0, 6, 12), True, 1, 512,
        third, operands, paced(third, 8.0, 4.8, 1.5), 2, "causal_fwd",
    )
    w_up, w_down = flat(whole)
    x2 = x1 + dg(o2, w_p, NN)
    normal_three, inverse_three = moments(x2)
    h3 = (normal_three * gain_three + bias_three).astype(BF16)
    up = dg(h3, w_up, NN)
    hidden = gelu(up).astype(BF16)
    x3 = x2 + dg(hidden, w_down, NN)
    block_out = jnp.where(padding, x3, 0.0).astype(BF16)

    dx3 = jnp.where(padding, cotangent[0].astype(F32), 0.0)
    dz = dx3.astype(BF16)
    dup = (dg(dz, w_down, NT) * gelu_slope(up)).astype(BF16)
    back, g_gain3, g_bias3 = norm_back(normal_three, inverse_three, gain_three, dg(dup, w_up, NT))
    dx2 = dx3 + back
    dy2 = dx2.astype(BF16)
    do2 = dg(dy2, w_p, NT).astype(BF16)
    fourth, operands = scatter([(weight(hidden, dz), (1, 0)), (weight(h3, dup), (0, 0))])
    (dqkv,), (s_up, s_down) = attn_bwd(
        clip_lengths, qkv, qkv, qkv, o2, do2, lse2, (0, 6, 12), True, 1, 256, 512,
        fourth, operands, paced(fourth, 8.0, 4.8, 2.45), 3, "causal_bwd",
    )
    dh2 = sum(dg(dqkv[c], w_qkv[:, c * D : (c + 1) * D], NT) for c in range(3))
    back, g_gain2, g_bias2 = norm_back(normal_two, inverse_two, gain_two, dh2)
    dx1 = dx2 + back
    dy1 = dx1.astype(BF16)
    do1 = dg(dy1, w_o, NT).astype(BF16)
    fifth, operands = scatter(
        [(weight(o2, dy2), (0, 0))]
        + [(weight(h2, dqkv[c]), (1, c * D)) for c in range(3)]
        + [(weight(o1, dy1), (2, 0))]
    )
    (dqkv1,), (s_p, s_qkv, s_o) = attn_bwd(
        context_frames, q1, k1, v1, o1, do1, lse1, (0, 0, 0), False, FRAME_TOK, 1024, 256,
        fifth, operands, paced(fifth, 8.0, 4.8, 3.1), 4, "cross_bwd",
    )
    dh1 = dg(dqkv1[0], w_q, NT)
    back, g_gain1, g_bias1 = norm_back(normal_one, inverse_one, gain_one, dh1)
    input_grad = dx1 + back

    g_norms = jnp.stack([g_gain1, g_bias1, g_gain2, g_bias2, g_gain3, g_bias3]).astype(BF16)
    g_norms = jnp.pad(g_norms.reshape(6, n, own).transpose(1, 0, 2), ((0, 0), (0, 10), (0, 256 - own)))

    sixth, operands = scatter(
        [
            (weight(context_rows, dqkv1[2]), (3, 0)),
            (weight(context_rows, dqkv1[1]), (2, 0)),
            (weight(h1, dqkv1[0]), (1, 0)),
            (g_norms, (0, 0)),
        ]
    )
    s_norms, s_q, s_k, s_v = alone(sixth, operands, 5, "scatter_cross")
    scale = (slot_rows * tokens.shape[0] * n * lax.axis_size("rep")) ** (-0.5)
    vec = [s_norms[i, :own] * scale for i in range(6)]
    done = [None, *finish([s_q, s_k, s_v, s_o, s_qkv, s_p, s_up, s_down], scale)]
    return (
        block_out[None],
        input_grad[None],
        vec[0],
        vec[1],
        done[1],
        done[2],
        done[3],
        done[4],
        vec[2],
        vec[3],
        done[5],
        done[6],
        vec[4],
        vec[5],
        done[7],
        done[8],
    )


def solution(mesh):
    in_specs = (
        P(("fsdp", "rep"), None, None),
        P(("fsdp", "rep"), None, None),
        P(("fsdp", "rep")),
        P(("fsdp", "rep")),
        P("fsdp"),
        P("fsdp"),
        P("fsdp", None),
        P("fsdp", None),
        P("fsdp", None),
        P("fsdp", None),
        P("fsdp"),
        P("fsdp"),
        P("fsdp", None),
        P("fsdp", None),
        P("fsdp"),
        P("fsdp"),
        P("fsdp", None),
        P("fsdp", None),
        P(("fsdp", "rep"), None, None),
    )
    out_specs = (
        P(("fsdp", "rep"), None, None),
        P(("fsdp", "rep"), None, None),
        P("fsdp"),
        P("fsdp"),
        P("fsdp", None),
        P("fsdp", None),
        P("fsdp", None),
        P("fsdp", None),
        P("fsdp"),
        P("fsdp"),
        P("fsdp", None),
        P("fsdp", None),
        P("fsdp"),
        P("fsdp"),
        P("fsdp", None),
        P("fsdp", None),
    )
    return jax.shard_map(shards, mesh=mesh, in_specs=in_specs, out_specs=out_specs, check_vma=False)
```

time: 534 us -> 504 us (0.944)
  Pallas kernels: 337 us -> 317 us
  local copies, waits for them, and re-layouts: 40.1 us -> 29.1 us
    pallas_call x6 -> x7, Pallas kernels: 337 us -> 317 us  [the longest x4 249 us: attend_beside(): pl.pallas_call(kernel, grid=(6,), in_specs=in_specs + [any_] * moved, out...]
    unnamed x98 -> x82, local copies, waits for them, and re-layouts: 28.3 us -> 18.5 us
where the time goes in v2:
time: 504 us; the launch traced here: 495 us
  Pallas kernels  317 us (63%)
  matrix products  119 us (24%)
  local copies, waits for them, and re-layouts  29.1 us (6%)
  other arithmetic  27.4 us (5%)
    pallas_call x4, Pallas kernels, attend_beside(): pl.pallas_call(kernel, grid=(6,), in_specs=in_specs + [any_] * moved, out...  249 us
    dot_general x26, matrix products, dg(): return lax.dot_general(a, b, dims, preferred_element_type=F32)  119 us
    pallas_call x2, Pallas kernels, alone(): pl.pallas_call(kernel, out_shape=engine.outs(), in_specs=[pl.BlockSpec(me...  65 us
    unnamed x82, local copies, waits for them, and re-layouts  18.5 us

profile of v2, /device:TPU:0, one launch (start us, length us, event | category | flops | bytes accessed | tf_op | source)
XLA Modules:
  0.0 495.3 jit_solution(2968902611414672449)
XLA Ops:
  8.5 34.2 %gather_cross.1 = (bf16[4,2,2,16,256]{4,3,2,1,0:T(8,128)(2,1)}, bf16[4,2,2,48,768]{4,3,2,1,0:T(8,128)(2,1)}, bf16[4,2,2,48,768]{4,3,2,1,0:T(8,128)(2,1)}, bf16[4,2,2,48,768]{4,3,2,1,0:T(8,128)(2,1)}) custom-call(bf16[16,256]{1,0:T(8,128)(2,1)} %pad.8.refs_0_, bf16[48,768]{1,0:T(8,128)(2,1)} %refs_1_.1, bf16[48,768]{1,0:T(8,128)(2,1)} %refs_2_.1, ...), custom_call_target="tpu_custom_call" | custom-call | tf_op jit(solution)/shard_map/gather_cross/pallas_call | solution.py:412
  44.1 4.2 convolution_convert_fusion.7.refs_1_
  53.4 52.1 %cross_fwd.1 = (bf16[1024,768]{1,0:T(8,128)(2,1)}, f32[6,2,1024]{2,1,0:T(2,128)}, bf16[4,2,2,48,768]{4,3,2,1,0:T(8,128)(2,1)}, bf16[4,2,2,48,2304]{4,3,2,1,0:T(8,128)(2,1)}, bf16[4,2,2,48,768]{4,3,2,1,0:T(8,128)(2,1)}) custom-call(s32[1]{0:T(128)S(6)} %copy.77.refs_0_, bf16[1024,768]{1,0:T(8,128)(2,1)} %convolution_convert_fusion.7.refs_1_, ...), custom_call_target="tpu_custom_call" | custom-call | tf_op jit(solution)/shard_map/cross_fwd/pallas_call | solution.py:483
  105.6 3.7 fusion.112
  113.0 5.7 %convolution_convert_fusion.refs_1_.refs_2_.refs_3_ = bf16[1024,2304]{1,0:T(8,128)(2,1)} fusion(bf16[1024,768]{0,1:T(8,128)(2,1)S(1)} %add_convert_fusion.1, bf16[768,2304]{1,0:T(8,128)(2,1)S(1)} %bitcast.200), kind=kOutput, calls=%fused_computation.11 | convolution fusion | flops 3626237952 | bytes 9830400 | tf_op jit(solution)/shard_map/dot_general | solution.py:20
  118.7 70.9 %causal_fwd.1 = (bf16[1024,768]{1,0:T(8,128)(2,1)}, f32[6,2,1024]{2,1,0:T(2,128)}, bf16[4,2,2,48,3072]{4,3,2,1,0:T(8,128)(2,1)}, bf16[4,2,2,192,768]{4,3,2,1,0:T(8,128)(2,1)}) custom-call(s32[1]{0:T(128)} %copy.76.refs_0_, bf16[1024,2304]{1,0:T(8,128)(2,1)} %convolution_convert_fusion.refs_1_.refs_2_.refs_3_, ...), custom_call_target="tpu_custom_call" | custom-call | tf_op jit(solution)/shard_map/causal_fwd/pallas_call | solution.py:483
  193.2 5.7 %fusion.111 = f32[1024,3072]{1,0:T(8,128)S(1)} fusion(bf16[768,3072]{1,0:T(8,128)(2,1)S(1)} %bitcast.188, f32[1024,768]{0,1:T(8,128)S(1)} %get-tuple-element.137, f32[768]{0:T(1024)S(1)} %add.109, f32[768]{0:T(1024)S(1)} %mul.252, f32[1024]{0:T(1024)S(1)} %add_rsqrt_fusion, f32[1024]{0:T(1024)S(1)} %broadcast_multiply_fusion.6), kind=kOutput, calls=%fused_computation.154 | convolution fusion | flops 4835770368 | bytes 20461568 | tf_op jit(solution)/shard_map/dot_general | solution.py:20
  198.9 4.6 copy-done.7
  203.5 9.2 %fusion.85 = bf16[1,1024,768]{1,2,0:T(8,128)(2,1)} fusion(f32[1024,768]{0,1:T(8,128)S(1)} %get-tuple-element.137, bf16[3072,768]{1,0:T(8,128)(2,1)} %bitcast.212, pred[1024]{0:T(1024)(128)(4,1)S(1)} %iota_compare_fusion, f32[1024,3072]{1,0:T(8,128)S(1)} %fusion.111), kind=kOutput, calls=%fused_computation.102 | convolution fusion | flops 4862509056 | bytes 22021120 | tf_op jit(solution)/shard_map/dot_general | solution.py:20
  215.4 15.7 %fusion.7 = bf16[1024,3072]{1,0:T(8,128)(2,1)} fusion(f32[1024,3072]{1,0:T(8,128)} %copy-done.7, bf16[3072,768]{1,0:T(8,128)(2,1)} %bitcast.213, bf16[1,1024,768]{1,2,0:T(8,128)(2,1)S(1)} %copy-done.11, pred[1024]{0:T(1024)(128)(4,1)S(1)} %iota_compare_fusion), kind=kOutput, calls=%fused_computation.9 | convolution fusion | flops 4893966336 | bytes 25166848 | tf_op jit(solution)/shard_map/dot_general | solution.py:20
  231.1 10.0 %convolution_convert_fusion.2 = bf16[3072,768]{1,0:T(8,128)(2,1)} fusion(bf16[1,1024,768]{1,2,0:T(8,128)(2,1)S(1)} %copy-done.11, pred[1024]{0:T(1024)(128)(4,1)S(1)} %iota_compare_fusion, f32[1024,3072]{1,0:T(8,128)S(1)} %copy-done.8), kind=kOutput, calls=%fused_computation.13 | convolution fusion | flops 4864868352 | bytes 18875392 | tf_op jit(solution)/shard_map/dot_general | solution.py:20
  241.2 9.2 %fusion.115 = (bf16[768]{0:T(1024)(128)(2,1)S(1)}, f32[1024,768]{1,0:T(8,128)}) fusion(bf16[1024,3072]{1,0:T(8,128)(2,1)S(1)} %copy-done.33, bf16[768,3072]{1,0:T(8,128)(2,1)} %bitcast.185), kind=kOutput, calls=%fused_computation.158 | convolution fusion | flops 4832623616 | bytes 14157312 | tf_op jit(solution)/shard_map/dot_general | solution.py:20
  250.4 7.2 %convolution_convert_fusion.1 = bf16[768,3072]{1,0:T(8,128)(2,1)} fusion(bf16[1024,3072]{1,0:T(8,128)(2,1)S(1)} %copy-done.33, f32[1024,768]{0,1:T(8,128)S(1)} %copy-done.2, f32[768]{0:T(1024)S(1)} %add.109, f32[768]{0:T(1024)S(1)} %mul.252, f32[1024]{0:T(1024)S(1)} %add_rsqrt_fusion, f32[1024]{0:T(1024)S(1)} %broadcast_multiply_fusion.6), kind=kOutput, calls=%fused_computation.12 | convolution fusion | flops 4838129664 | bytes 14170112 | tf_op jit(solution)/shard_map/dot_general | solution.py:20
  257.6 3.9 copy.54
  261.5 3.8 multiply_reduce_fusion
  265.5 4.5 fusion.24
  272.6 66.7 %causal_bwd.1 = (bf16[3,1024,768]{2,1,0:T(8,128)(2,1)}, f32[48,3072]{1,0:T(8,128)}, f32[192,768]{1,0:T(8,128)}) custom-call(s32[1]{0:T(128)} %copy.76.refs_0_, bf16[1024,2304]{1,0:T(8,128)(2,1)} %convolution_convert_fusion.refs_1_.refs_2_.refs_3_, bf16[1024,2304]{1,0:T(8,128)(2,1)} %convolution_convert_fusion.refs_1_.refs_2_.refs_3_, ...), custom_call_target="tpu_custom_call" | custom-call | tf_op jit(solution)/shard_map/causal_bwd/pallas_call | solution.py:483
  339.3 4.0 convolution_convert_fusion.9
  357.6 6.4 %multiply_add_fusion.1 = f32[1024,768]{0,1:T(8,128)} fusion(f32[1024,768]{0,1:T(8,128)} %copy-done.10, f32[1024,768]{0,1:T(8,128)} %get-tuple-element.138, f32[1024,768]{0,1:T(8,128)} %copy-done.3, f32[1024]{0:T(1024)S(1)} %broadcast_multiply_fusion.2, f32[1024]{0:T(1024)S(1)} %broadcast_multiply_fusion.3, f32[768]{0:T(1024)S(1)} %mul.246, ...), kind=kLoop, calls=%fused_computation.43 | loop fusion | flops 6291456 | bytes 12602368 | tf_op jit(solution)/shard_map/add | solution.py:684
  364.2 4.7 convolution_convert_fusion.5.refs_5_
  371.4 59.0 %cross_bwd.1 = (bf16[3,1024,768]{2,1,0:T(8,128)(2,1)}, f32[48,768]{1,0:T(8,128)}, f32[48,2304]{1,0:T(8,128)}, f32[48,768]{1,0:T(8,128)}) custom-call(s32[1]{0:T(128)S(6)} %copy.77.refs_0_, bf16[1024,768]{1,0:T(8,128)(2,1)} %convolution_convert_fusion.7.refs_1_, bf16[1024,768]{1,0:T(8,128)(2,1)} %fusion.86.refs_2_, bf16[1024,768]{1,0:T(8,128)(2,1)} %fusion.89.refs_3_, ...), custom_call_target="tpu_custom_call" | custom-call | tf_op jit(solution)/shard_map/cross_bwd/pallas_call | solution.py:483
  430.4 4.2 fusion.72
  449.6 5.5 %fusion.19 = f32[1,1024,768]{1,2,0:T(8,128)} fusion(f32[1024,768]{0,1:T(8,128)} %multiply_add_fusion.1, bf16[1,1024,768]{1,2,0:T(8,128)(2,1)S(1)} %copy-done.6, f32[1024,768]{0,1:T(8,128)} %copy.58, f32[1024]{0:T(1024)S(1)} %broadcast_multiply_fusion, f32[1024]{0:T(1024)S(1)} %broadcast_multiply_fusion.1, f32[768]{0:T(1024)S(1)} %copy-done.23, ...), kind=kLoop, calls=%fused_computation.30 | loop fusion | flops 7077888 | bytes 11029504 | tf_op jit(solution)/shard_map/broadcast_in_dim | solution.py:717
  459.4 30.8 %scatter_cross.1 = (f32[16,256]{1,0:T(8,128)}, f32[48,768]{1,0:T(8,128)}, f32[48,768]{1,0:T(8,128)}, f32[48,768]{1,0:T(8,128)}) custom-call(bf16[4,2,2,48,768]{4,3,2,1,0:T(8,128)(2,1)} %bitcast.191, bf16[4,2,2,48,768]{4,3,2,1,0:T(8,128)(2,1)} %bitcast.190, bf16[4,2,2,48,768]{4,3,2,1,0:T(8,128)(2,1)} %bitcast.189, bf16[4,2,2,16,256]{4,3,2,1,0:T(8,128)(2,1)} %bitcast.199), custom_call_target="tpu_custom_call" | custom-call | tf_op jit(solution)/shard_map/scatter_cross/pallas_call | solution.py:412
  (135 shorter events, 66.3 us)
Async XLA Ops:
  0.6 47.7 %copy-start = (bf16[1,1024,768]{2,1,0:T(8,128)(2,1)S(1)}, bf16[1,1024,768]{2,1,0:T(8,128)(2,1)}, u32[]{:S(2)}) copy-start(bf16[1,1024,768]{2,1,0:T(8,128)(2,1)} %param.20) | copy-start | bytes 4718596
  5.2 38.9 %copy-start.5 = (bf16[1,1024,768]{1,2,0:T(8,128)(2,1)}, bf16[1,1024,768]{1,2,0:T(8,128)(2,1)S(1)}, u32[]{:S(2)}) copy-start(bf16[1,1024,768]{1,2,0:T(8,128)(2,1)S(1)} %copy.49) | copy-start | bytes 4718596
  5.5 42.8 %copy-start.20 = (f32[1024]{0:T(1024)}, f32[1024]{0:T(1024)S(1)}, u32[]{:S(2)}) copy-start(f32[1024]{0:T(1024)S(1)} %broadcast_multiply_fusion.8) | copy-start | bytes 12292
  5.9 42.4 %copy-start.24 = (f32[1024]{0:T(1024)}, f32[1024]{0:T(1024)S(1)}, u32[]{:S(2)}) copy-start(f32[1024]{0:T(1024)S(1)} %add_rsqrt_fusion.2) | copy-start | bytes 12292
  43.8 4.5 copy-start.22
  44.0 4.3 copy-start.26
  44.1 4.3 copy-start.32
  109.3 80.3 %copy-start.3 = (f32[1024,768]{0,1:T(8,128)}, f32[1024,768]{0,1:T(8,128)S(1)}, u32[]{:S(2)}) copy-start(f32[1024,768]{0,1:T(8,128)S(1)} %get-tuple-element.135) | copy-start | bytes 9437188
  118.7 71.0 %copy-start.15 = (bf16[4,2,2,48,768]{4,3,2,1,0:T(8,128)(2,1)S(1)}, bf16[4,2,2,48,768]{4,3,2,1,0:T(8,128)(2,1)}, u32[]{:S(2)}) copy-start(bf16[4,2,2,48,768]{4,3,2,1,0:T(8,128)(2,1)} %get-tuple-element.56) | copy-start | bytes 3538948
  192.8 6.1 %copy-start.1 = (f32[1024,768]{0,1:T(8,128)}, f32[1024,768]{0,1:T(8,128)S(1)}, u32[]{:S(2)}) copy-start(f32[1024,768]{0,1:T(8,128)S(1)} %get-tuple-element.137) | copy-start | bytes 9437188
  198.9 4.6 copy-start.7
  215.4 15.7 %copy-start.8 = (f32[1024,3072]{1,0:T(8,128)S(1)}, f32[1024,3072]{1,0:T(8,128)}, u32[]{:S(2)}) copy-start(f32[1024,3072]{1,0:T(8,128)} %copy-done.7) | copy-start | bytes 37748740
  231.1 10.0 %copy-start.33 = (bf16[1024,3072]{1,0:T(8,128)(2,1)S(1)}, bf16[1024,3072]{1,0:T(8,128)(2,1)}, u32[]{:S(2)}) copy-start(bf16[1024,3072]{1,0:T(8,128)(2,1)} %fusion.7) | copy-start | bytes 18874372
  241.2 9.2 %copy-start.2 = (f32[1024,768]{0,1:T(8,128)S(1)}, f32[1024,768]{0,1:T(8,128)}, u32[]{:S(2)}) copy-start(f32[1024,768]{0,1:T(8,128)} %copy-done.1) | copy-start | bytes 9437188
  265.5 4.5 copy-start.16
  270.0 69.4 %copy-start.10 = (f32[1024,768]{0,1:T(8,128)}, f32[1024,768]{0,1:T(8,128)S(1)}, u32[]{:S(2)}) copy-start(f32[1024,768]{0,1:T(8,128)S(1)} %fusion.24) | copy-start | bytes 9437188
  357.6 6.5 %copy-start.30 = (bf16[4,2,2,48,768]{4,3,2,1,0:T(8,128)(2,1)S(1)}, bf16[4,2,2,48,768]{4,3,2,1,0:T(8,128)(2,1)}, u32[]{:S(2)}) copy-start(bf16[4,2,2,48,768]{4,3,2,1,0:T(8,128)(2,1)} %get-tuple-element.53) | copy-start | bytes 3538948
  364.2 4.7 copy-start.9
  364.2 4.7 copy-start.14
  371.3 59.1 %copy-start.6 = (bf16[1,1024,768]{1,2,0:T(8,128)(2,1)S(1)}, bf16[1,1024,768]{1,2,0:T(8,128)(2,1)}, u32[]{:S(2)}) copy-start(bf16[1,1024,768]{1,2,0:T(8,128)(2,1)} %copy-done.5) | copy-start | bytes 4718596
  371.3 59.1 %copy-start.21 = (f32[1024]{0:T(1024)S(1)}, f32[1024]{0:T(1024)}, u32[]{:S(2)}) copy-start(f32[1024]{0:T(1024)} %copy-done.20) | copy-start | bytes 12292
  371.3 59.1 %copy-start.23 = (f32[768]{0:T(1024)S(1)}, f32[768]{0:T(1024)}, u32[]{:S(2)}) copy-start(f32[768]{0:T(1024)} %copy-done.22) | copy-start | bytes 9220
  371.3 59.1 %copy-start.25 = (f32[1024]{0:T(1024)S(1)}, f32[1024]{0:T(1024)}, u32[]{:S(2)}) copy-start(f32[1024]{0:T(1024)} %copy-done.24) | copy-start | bytes 12292
  371.3 59.1 %copy-start.27 = (f32[768]{0:T(1024)S(1)}, f32[768]{0:T(1024)}, u32[]{:S(2)}) copy-start(f32[768]{0:T(1024)} %copy-done.26) | copy-start | bytes 9220
  (12 other events, 36.0 us)

commit v3 on v2

--- a/solution.py
+++ b/solution.py
@@ -161,6 +161,9 @@
             action(1, "y", "x")
 
 
+AHEAD = 3
+
+
 class Gather:
     def __init__(self, shapes, n):
         self.dims = grid_of(n)
@@ -176,7 +179,7 @@
         Z, Y, X = self.dims
         M, z, s = len(self.pieces), max(self.dims[0] - 1, 1), max(Y - 1, X - 1, 1)
         sem = pltpu.SemaphoreType.DMA
-        return [sem((self.count,))] + [sem((M, c)) for c in (z, z, s, s, s, s, z, z, s, s, s, s)]
+        return [sem((2, self.count))] + [sem((M, c)) for c in (z, z, s, s, s, s, z, z, s, s, s, s)]
 
     def bind(self, shards, outs, scratch):
         self.shards, self.out = shards, outs
@@ -218,7 +221,7 @@
     def own_copies(self):
         p = self.place.mine
         return [
-            pltpu.make_async_copy(s, o.at[p["z"], p["y"], p["x"]], self.own.at[i])
+            remote(s, o.at[p["z"], p["y"], p["x"]], self.own.at[0, i], self.own.at[1, i], self.place.sibling())
             for i, (s, o) in enumerate(zip(self.shards, self.out))
         ]
 
@@ -227,7 +230,7 @@
             c.start()
 
         def go(core, a, b):
-            for m in range(len(self.pieces)):
+            for m in range(min(AHEAD, len(self.pieces))):
                 for _, c in self.hop(0, m, core, (a, b), False):
                     c().start()
 
@@ -239,6 +242,9 @@
                 c.wait()
 
         def go(core, a, b):
+            if t + AHEAD < len(self.pieces):
+                for _, c in self.hop(0, t + AHEAD, core, (a, b), False):
+                    c().start()
             for stage in range(3):
                 m = t - stage
                 if not 0 <= m < len(self.pieces):

time: 504 us -> 493 us (0.978)
  Pallas kernels: 317 us -> 306 us
    pallas_call x4, Pallas kernels: 249 us -> 237 us  [attend_beside(): pl.pallas_call(kernel, grid=(6,), in_specs=in_specs + [any_] * moved, out...]
where the time goes in v3:
time: 493 us; the launch traced here: 484 us
  Pallas kernels  306 us (62%)
  matrix products  119 us (24%)
  local copies, waits for them, and re-layouts  29.1 us (6%)
  other arithmetic  27.4 us (6%)
    pallas_call x4, Pallas kernels, attend_beside(): pl.pallas_call(kernel, grid=(6,), in_specs=in_specs + [any_] * moved, out...  237 us
    dot_general x26, matrix products, dg(): return lax.dot_general(a, b, dims, preferred_element_type=F32)  119 us
    pallas_call x2, Pallas kernels, alone(): pl.pallas_call(kernel, out_shape=engine.outs(), in_specs=[pl.BlockSpec(me...  65.1 us
    unnamed x82, local copies, waits for them, and re-layouts  18.5 us

profile of v3, /device:TPU:0, one launch (start us, length us, event | category | flops | bytes accessed | tf_op | source)
XLA Modules:
  0.0 484.0 jit_solution(182229542192340215)
XLA Ops:
  8.5 32.9 %gather_cross.1 = (bf16[4,2,2,16,256]{4,3,2,1,0:T(8,128)(2,1)}, bf16[4,2,2,48,768]{4,3,2,1,0:T(8,128)(2,1)}, bf16[4,2,2,48,768]{4,3,2,1,0:T(8,128)(2,1)}, bf16[4,2,2,48,768]{4,3,2,1,0:T(8,128)(2,1)}) custom-call(bf16[16,256]{1,0:T(8,128)(2,1)} %pad.8.refs_0_, bf16[48,768]{1,0:T(8,128)(2,1)} %refs_1_.1, bf16[48,768]{1,0:T(8,128)(2,1)} %refs_2_.1, ...), custom_call_target="tpu_custom_call" | custom-call | tf_op jit(solution)/shard_map/gather_cross/pallas_call | solution.py:418
  42.8 4.2 convolution_convert_fusion.7.refs_1_
  52.2 50.4 %cross_fwd.1 = (bf16[1024,768]{1,0:T(8,128)(2,1)}, f32[6,2,1024]{2,1,0:T(2,128)}, bf16[4,2,2,48,768]{4,3,2,1,0:T(8,128)(2,1)}, bf16[4,2,2,48,2304]{4,3,2,1,0:T(8,128)(2,1)}, bf16[4,2,2,48,768]{4,3,2,1,0:T(8,128)(2,1)}) custom-call(s32[1]{0:T(128)S(6)} %copy.77.refs_0_, bf16[1024,768]{1,0:T(8,128)(2,1)} %convolution_convert_fusion.7.refs_1_, ...), custom_call_target="tpu_custom_call" | custom-call | tf_op jit(solution)/shard_map/cross_fwd/pallas_call | solution.py:489
  102.6 3.7 fusion.112
  110.0 5.7 %convolution_convert_fusion.refs_1_.refs_2_.refs_3_ = bf16[1024,2304]{1,0:T(8,128)(2,1)} fusion(bf16[1024,768]{0,1:T(8,128)(2,1)S(1)} %add_convert_fusion.1, bf16[768,2304]{1,0:T(8,128)(2,1)S(1)} %bitcast.200), kind=kOutput, calls=%fused_computation.11 | convolution fusion | flops 3626237952 | bytes 9830400 | tf_op jit(solution)/shard_map/dot_general | solution.py:20
  115.7 60.9 %causal_fwd.1 = (bf16[1024,768]{1,0:T(8,128)(2,1)}, f32[6,2,1024]{2,1,0:T(2,128)}, bf16[4,2,2,48,3072]{4,3,2,1,0:T(8,128)(2,1)}, bf16[4,2,2,192,768]{4,3,2,1,0:T(8,128)(2,1)}) custom-call(s32[1]{0:T(128)} %copy.76.refs_0_, bf16[1024,2304]{1,0:T(8,128)(2,1)} %convolution_convert_fusion.refs_1_.refs_2_.refs_3_, ...), custom_call_target="tpu_custom_call" | custom-call | tf_op jit(solution)/shard_map/causal_fwd/pallas_call | solution.py:489
  180.2 5.7 %fusion.111 = f32[1024,3072]{1,0:T(8,128)S(1)} fusion(bf16[768,3072]{1,0:T(8,128)(2,1)S(1)} %bitcast.188, f32[1024,768]{0,1:T(8,128)S(1)} %get-tuple-element.137, f32[768]{0:T(1024)S(1)} %add.109, f32[768]{0:T(1024)S(1)} %mul.252, f32[1024]{0:T(1024)S(1)} %add_rsqrt_fusion, f32[1024]{0:T(1024)S(1)} %broadcast_multiply_fusion.6), kind=kOutput, calls=%fused_computation.154 | convolution fusion | flops 4835770368 | bytes 20461568 | tf_op jit(solution)/shard_map/dot_general | solution.py:20
  185.9 4.6 copy-done.7
  190.5 9.2 %fusion.85 = bf16[1,1024,768]{1,2,0:T(8,128)(2,1)} fusion(f32[1024,768]{0,1:T(8,128)S(1)} %get-tuple-element.137, bf16[3072,768]{1,0:T(8,128)(2,1)} %bitcast.212, pred[1024]{0:T(1024)(128)(4,1)S(1)} %iota_compare_fusion, f32[1024,3072]{1,0:T(8,128)S(1)} %fusion.111), kind=kOutput, calls=%fused_computation.102 | convolution fusion | flops 4862509056 | bytes 22021120 | tf_op jit(solution)/shard_map/dot_general | solution.py:20
  202.4 15.7 %fusion.7 = bf16[1024,3072]{1,0:T(8,128)(2,1)} fusion(f32[1024,3072]{1,0:T(8,128)} %copy-done.7, bf16[3072,768]{1,0:T(8,128)(2,1)} %bitcast.213, bf16[1,1024,768]{1,2,0:T(8,128)(2,1)S(1)} %copy-done.11, pred[1024]{0:T(1024)(128)(4,1)S(1)} %iota_compare_fusion), kind=kOutput, calls=%fused_computation.9 | convolution fusion | flops 4893966336 | bytes 25166848 | tf_op jit(solution)/shard_map/dot_general | solution.py:20
  218.1 10.0 %convolution_convert_fusion.2 = bf16[3072,768]{1,0:T(8,128)(2,1)} fusion(bf16[1,1024,768]{1,2,0:T(8,128)(2,1)S(1)} %copy-done.11, pred[1024]{0:T(1024)(128)(4,1)S(1)} %iota_compare_fusion, f32[1024,3072]{1,0:T(8,128)S(1)} %copy-done.8), kind=kOutput, calls=%fused_computation.13 | convolution fusion | flops 4864868352 | bytes 18875392 | tf_op jit(solution)/shard_map/dot_general | solution.py:20
  228.2 9.2 %fusion.115 = (bf16[768]{0:T(1024)(128)(2,1)S(1)}, f32[1024,768]{1,0:T(8,128)}) fusion(bf16[1024,3072]{1,0:T(8,128)(2,1)S(1)} %copy-done.33, bf16[768,3072]{1,0:T(8,128)(2,1)} %bitcast.185), kind=kOutput, calls=%fused_computation.158 | convolution fusion | flops 4832623616 | bytes 14157312 | tf_op jit(solution)/shard_map/dot_general | solution.py:20
  237.4 7.2 %convolution_convert_fusion.1 = bf16[768,3072]{1,0:T(8,128)(2,1)} fusion(bf16[1024,3072]{1,0:T(8,128)(2,1)S(1)} %copy-done.33, f32[1024,768]{0,1:T(8,128)S(1)} %copy-done.2, f32[768]{0:T(1024)S(1)} %add.109, f32[768]{0:T(1024)S(1)} %mul.252, f32[1024]{0:T(1024)S(1)} %add_rsqrt_fusion, f32[1024]{0:T(1024)S(1)} %broadcast_multiply_fusion.6), kind=kOutput, calls=%fused_computation.12 | convolution fusion | flops 4838129664 | bytes 14170112 | tf_op jit(solution)/shard_map/dot_general | solution.py:20
  244.6 3.9 copy.54
  248.5 3.8 multiply_reduce_fusion
  252.5 4.5 fusion.24
  259.6 67.2 %causal_bwd.1 = (bf16[3,1024,768]{2,1,0:T(8,128)(2,1)}, f32[48,3072]{1,0:T(8,128)}, f32[192,768]{1,0:T(8,128)}) custom-call(s32[1]{0:T(128)} %copy.76.refs_0_, bf16[1024,2304]{1,0:T(8,128)(2,1)} %convolution_convert_fusion.refs_1_.refs_2_.refs_3_, bf16[1024,2304]{1,0:T(8,128)(2,1)} %convolution_convert_fusion.refs_1_.refs_2_.refs_3_, ...), custom_call_target="tpu_custom_call" | custom-call | tf_op jit(solution)/shard_map/causal_bwd/pallas_call | solution.py:489
  326.8 4.0 convolution_convert_fusion.9
  345.1 6.4 %multiply_add_fusion.1 = f32[1024,768]{0,1:T(8,128)} fusion(f32[1024,768]{0,1:T(8,128)} %copy-done.10, f32[1024,768]{0,1:T(8,128)} %get-tuple-element.138, f32[1024,768]{0,1:T(8,128)} %copy-done.3, f32[1024]{0:T(1024)S(1)} %broadcast_multiply_fusion.2, f32[1024]{0:T(1024)S(1)} %broadcast_multiply_fusion.3, f32[768]{0:T(1024)S(1)} %mul.246, ...), kind=kLoop, calls=%fused_computation.43 | loop fusion | flops 6291456 | bytes 12602368 | tf_op jit(solution)/shard_map/add | solution.py:690
  351.7 4.7 convolution_convert_fusion.5.refs_5_
  358.8 58.8 %cross_bwd.1 = (bf16[3,1024,768]{2,1,0:T(8,128)(2,1)}, f32[48,768]{1,0:T(8,128)}, f32[48,2304]{1,0:T(8,128)}, f32[48,768]{1,0:T(8,128)}) custom-call(s32[1]{0:T(128)S(6)} %copy.77.refs_0_, bf16[1024,768]{1,0:T(8,128)(2,1)} %convolution_convert_fusion.7.refs_1_, bf16[1024,768]{1,0:T(8,128)(2,1)} %fusion.86.refs_2_, bf16[1024,768]{1,0:T(8,128)(2,1)} %fusion.89.refs_3_, ...), custom_call_target="tpu_custom_call" | custom-call | tf_op jit(solution)/shard_map/cross_bwd/pallas_call | solution.py:489
  417.7 4.2 fusion.72
  436.8 5.5 %fusion.19 = f32[1,1024,768]{1,2,0:T(8,128)} fusion(f32[1024,768]{0,1:T(8,128)} %multiply_add_fusion.1, bf16[1,1024,768]{1,2,0:T(8,128)(2,1)S(1)} %copy-done.6, f32[1024,768]{0,1:T(8,128)} %copy.58, f32[1024]{0:T(1024)S(1)} %broadcast_multiply_fusion, f32[1024]{0:T(1024)S(1)} %broadcast_multiply_fusion.1, f32[768]{0:T(1024)S(1)} %copy-done.23, ...), kind=kLoop, calls=%fused_computation.30 | loop fusion | flops 7077888 | bytes 11029504 | tf_op jit(solution)/shard_map/broadcast_in_dim | solution.py:723
  446.6 32.2 %scatter_cross.1 = (f32[16,256]{1,0:T(8,128)}, f32[48,768]{1,0:T(8,128)}, f32[48,768]{1,0:T(8,128)}, f32[48,768]{1,0:T(8,128)}) custom-call(bf16[4,2,2,48,768]{4,3,2,1,0:T(8,128)(2,1)} %bitcast.191, bf16[4,2,2,48,768]{4,3,2,1,0:T(8,128)(2,1)} %bitcast.190, bf16[4,2,2,48,768]{4,3,2,1,0:T(8,128)(2,1)} %bitcast.189, bf16[4,2,2,16,256]{4,3,2,1,0:T(8,128)(2,1)} %bitcast.199), custom_call_target="tpu_custom_call" | custom-call | tf_op jit(solution)/shard_map/scatter_cross/pallas_call | solution.py:418
  (135 shorter events, 66.3 us)
Async XLA Ops:
  0.6 46.4 %copy-start = (bf16[1,1024,768]{2,1,0:T(8,128)(2,1)S(1)}, bf16[1,1024,768]{2,1,0:T(8,128)(2,1)}, u32[]{:S(2)}) copy-start(bf16[1,1024,768]{2,1,0:T(8,128)(2,1)} %param.20) | copy-start | bytes 4718596
  5.2 37.6 %copy-start.5 = (bf16[1,1024,768]{1,2,0:T(8,128)(2,1)}, bf16[1,1024,768]{1,2,0:T(8,128)(2,1)S(1)}, u32[]{:S(2)}) copy-start(bf16[1,1024,768]{1,2,0:T(8,128)(2,1)S(1)} %copy.49) | copy-start | bytes 4718596
  5.5 41.6 %copy-start.20 = (f32[1024]{0:T(1024)}, f32[1024]{0:T(1024)S(1)}, u32[]{:S(2)}) copy-start(f32[1024]{0:T(1024)S(1)} %broadcast_multiply_fusion.8) | copy-start | bytes 12292
  5.9 41.1 %copy-start.24 = (f32[1024]{0:T(1024)}, f32[1024]{0:T(1024)S(1)}, u32[]{:S(2)}) copy-start(f32[1024]{0:T(1024)S(1)} %add_rsqrt_fusion.2) | copy-start | bytes 12292
  42.5 4.5 copy-start.22
  42.7 4.3 copy-start.26
  42.8 4.3 copy-start.32
  106.4 70.3 %copy-start.3 = (f32[1024,768]{0,1:T(8,128)}, f32[1024,768]{0,1:T(8,128)S(1)}, u32[]{:S(2)}) copy-start(f32[1024,768]{0,1:T(8,128)S(1)} %get-tuple-element.135) | copy-start | bytes 9437188
  115.7 60.9 %copy-start.15 = (bf16[4,2,2,48,768]{4,3,2,1,0:T(8,128)(2,1)S(1)}, bf16[4,2,2,48,768]{4,3,2,1,0:T(8,128)(2,1)}, u32[]{:S(2)}) copy-start(bf16[4,2,2,48,768]{4,3,2,1,0:T(8,128)(2,1)} %get-tuple-element.56) | copy-start | bytes 3538948
  179.8 6.1 %copy-start.1 = (f32[1024,768]{0,1:T(8,128)}, f32[1024,768]{0,1:T(8,128)S(1)}, u32[]{:S(2)}) copy-start(f32[1024,768]{0,1:T(8,128)S(1)} %get-tuple-element.137) | copy-start | bytes 9437188
  185.9 4.6 copy-start.7
  202.4 15.7 %copy-start.8 = (f32[1024,3072]{1,0:T(8,128)S(1)}, f32[1024,3072]{1,0:T(8,128)}, u32[]{:S(2)}) copy-start(f32[1024,3072]{1,0:T(8,128)} %copy-done.7) | copy-start | bytes 37748740
  218.1 10.0 %copy-start.33 = (bf16[1024,3072]{1,0:T(8,128)(2,1)S(1)}, bf16[1024,3072]{1,0:T(8,128)(2,1)}, u32[]{:S(2)}) copy-start(bf16[1024,3072]{1,0:T(8,128)(2,1)} %fusion.7) | copy-start | bytes 18874372
  228.2 9.2 %copy-start.2 = (f32[1024,768]{0,1:T(8,128)S(1)}, f32[1024,768]{0,1:T(8,128)}, u32[]{:S(2)}) copy-start(f32[1024,768]{0,1:T(8,128)} %copy-done.1) | copy-start | bytes 9437188
  252.5 4.5 copy-start.16
  257.0 69.9 %copy-start.10 = (f32[1024,768]{0,1:T(8,128)}, f32[1024,768]{0,1:T(8,128)S(1)}, u32[]{:S(2)}) copy-start(f32[1024,768]{0,1:T(8,128)S(1)} %fusion.24) | copy-start | bytes 9437188
  345.1 6.5 %copy-start.30 = (bf16[4,2,2,48,768]{4,3,2,1,0:T(8,128)(2,1)S(1)}, bf16[4,2,2,48,768]{4,3,2,1,0:T(8,128)(2,1)}, u32[]{:S(2)}) copy-start(bf16[4,2,2,48,768]{4,3,2,1,0:T(8,128)(2,1)} %get-tuple-element.53) | copy-start | bytes 3538948
  351.6 4.7 copy-start.9
  351.7 4.7 copy-start.14
  358.8 58.8 %copy-start.6 = (bf16[1,1024,768]{1,2,0:T(8,128)(2,1)S(1)}, bf16[1,1024,768]{1,2,0:T(8,128)(2,1)}, u32[]{:S(2)}) copy-start(bf16[1,1024,768]{1,2,0:T(8,128)(2,1)} %copy-done.5) | copy-start | bytes 4718596
  358.8 58.8 %copy-start.21 = (f32[1024]{0:T(1024)S(1)}, f32[1024]{0:T(1024)}, u32[]{:S(2)}) copy-start(f32[1024]{0:T(1024)} %copy-done.20) | copy-start | bytes 12292
  358.8 58.8 %copy-start.23 = (f32[768]{0:T(1024)S(1)}, f32[768]{0:T(1024)}, u32[]{:S(2)}) copy-start(f32[768]{0:T(1024)} %copy-done.22) | copy-start | bytes 9220
  358.8 58.8 %copy-start.25 = (f32[1024]{0:T(1024)S(1)}, f32[1024]{0:T(1024)}, u32[]{:S(2)}) copy-start(f32[1024]{0:T(1024)} %copy-done.24) | copy-start | bytes 12292
  358.8 58.8 %copy-start.27 = (f32[768]{0:T(1024)S(1)}, f32[768]{0:T(1024)}, u32[]{:S(2)}) copy-start(f32[768]{0:T(1024)} %copy-done.26) | copy-start | bytes 9220
  (12 other events, 36.0 us)

commit v4 on v3

--- a/solution.py
+++ b/solution.py
@@ -27,7 +27,7 @@
     ka = jnp.where(mine, k2, jnp.where(extra, bias, 0.0).astype(BF16))
     return qa, ka
 
-def fwd_kernel(n_ref, q_ref, k_ref, v_ref, o_ref, l_ref, vt, *, causal, bq, unit, at):
+def fwd_kernel(n_ref, q_ref, k_ref, v_ref, o_ref, l_ref, vt, ot, *, causal, bq, unit, at):
     T = q_ref.shape[0]; K = k_ref.shape[0]
     live = n_ref[0] * unit
     bias = jnp.where(lax.broadcasted_iota(jnp.int32, (K, 1), 0) < live, 0.0, -1e30).astype(F32)
@@ -49,9 +49,9 @@
             m = jnp.max(s, 0, keepdims=True)
             p = jnp.exp(s - m)
             l = jnp.sum(p, 0, keepdims=True)
-            ot = dg(vt[side * 64:(side + 1) * 64, :span], p.astype(BF16), NN) * (1.0 / l)
-            o_ref[j * bq:(j + 1) * bq, side * 64:(side + 1) * 64] = ot.T.astype(BF16)
+            ot[side * 64:(side + 1) * 64, j * bq:(j + 1) * bq] = dg(vt[side * 64:(side + 1) * 64, :span], p.astype(BF16), NN) * (1.0 / l)
             l_ref[0, side:side + 1, j * bq:(j + 1) * bq] = m + jnp.log(l)
+    o_ref[...] = ot[...].T.astype(BF16)
 
 
 def bwd_kernel(n_ref, q_ref, k_ref, v_ref, o_ref, do_ref, l_ref, g_ref, kt, dqt, dka, dva, *, causal, bq, bk, unit, at):
@@ -260,18 +260,29 @@
 
         self.place.by_core(go)
 
-    def end(self):
+    def arrive(self, pieces):
+        def go(core, a, b):
+            for m in pieces:
+                for stage in range(3):
+                    for k, (at, _) in enumerate(self.hop(stage, m, core, (b, a), True)):
+                        self.give(stage, m, 1 - core, at, k).wait_recv()
+
+        self.place.by_core(go)
+
+    def sent(self):
         def go(core, a, b):
             for m in range(len(self.pieces)):
                 for stage in range(3):
-                    for k, (at, c) in enumerate(self.hop(stage, m, core, (a, b), False)):
+                    for _, c in self.hop(stage, m, core, (a, b), False):
                         c().wait_send()
                     for k, (at, _) in enumerate(self.hop(stage, m, core, (a, b), True)):
                         self.give(stage, m, core, at, k).wait_send()
-                    for k, (at, _) in enumerate(self.hop(stage, m, core, (b, a), True)):
-                        self.give(stage, m, 1 - core, at, k).wait_recv()
 
         self.place.by_core(go)
+
+    def end(self):
+        self.arrive(range(len(self.pieces)))
+        self.sent()
 
 
 class Scatter:
@@ -515,7 +526,7 @@
         ],
         [jax.ShapeDtypeStruct((T, D), BF16), jax.ShapeDtypeStruct((6, 2, T), F32)],
         [pl.BlockSpec((T, 128), lambda i: (0, i)), pl.BlockSpec((1, 2, T), lambda i: (i, 0, 0))],
-        [pltpu.VMEM((128, K), BF16)],
+        [pltpu.VMEM((128, K), BF16), pltpu.VMEM((128, T), F32)],
         engine,
         operands,
         points,
@@ -592,6 +603,204 @@
 def gelu_slope(u):
     t = jnp.tanh(GELU_A * (u + GELU_B * u * u * u))
     return 0.5 * (1.0 + t) + 0.5 * u * (1.0 - t * t) * (GELU_A * (1.0 + 3.0 * GELU_B * u * u))
+
+
+def blocks(rows, step, body):
+    def go(r, _):
+        body(pl.ds(pl.multiple_of(r * step, step), step))
+        return 0
+
+    lax.fori_loop(0, rows // step, go, 0)
+
+
+def pair(ref, i, first=0):
+    return ref.at[:, pl.ds(pl.multiple_of(first + i * 128, 128), 128)]
+
+
+def norm_rows(packed):
+    count = packed.shape[0]
+    own = D // count
+    total = None
+    for j in range(count):
+        r = lax.broadcasted_iota(jnp.int32, (128, D), 0)
+        c = lax.broadcasted_iota(jnp.int32, (128, D), 1)
+        spot = jnp.where((c == r + own * j) & (r < own), 1.0, 0.0).astype(BF16)
+        part = dg(packed[j, :, :128], spot, NN)
+        total = part if total is None else total + part
+    return total
+
+
+def forward_kernel(eng, ticks_cross, ticks_causal, *refs):
+    it = iter(refs)
+
+    def take(count):
+        return [next(it) for _ in range(count)]
+
+    clip, frames, tok_in, ctx_in = take(4)
+    shards = take(eng.count)
+    whole = take(eng.count)
+    q1_o, k1_o, v1_o, o1_o, h1_o, x1_o, h2_o, qkv_o, o2_o, x2_o, h3_o, lse1_o, lse2_o, norms_o = take(14)
+    tok, ctx, q1, k1, v1, o1, h1, x1, h2, qkv, o2, x2, h3, lse1, lse2, norms = take(16)
+    packed, wa, wb, wqkv, vt, ot, isem, wsem, osem = take(9)
+    eng.bind(shards, whole, list(it))
+    T = tok.shape[0]
+    eng.place.greet()
+    eng.begin()
+    loads = [pltpu.make_async_copy(ctx_in, ctx, isem.at[0]), pltpu.make_async_copy(tok_in, tok, isem.at[1])]
+    for c in loads:
+        c.start()
+    saves = []
+
+    def save(ref, out):
+        c = pltpu.make_async_copy(ref, out, osem.at[len(saves)])
+        c.start()
+        saves.append(c)
+
+    def fetch(i, pieces, ref):
+        eng.arrive(pieces)
+        c = pltpu.make_async_copy(whole[i], ref, wsem)
+        c.start()
+        c.wait()
+
+    def matrix(ref, c=0):
+        return ref[:, :, :, :, c : c + D].reshape(D, D)
+
+    for t in range(3):
+        eng.step(t)
+    fetch(0, [0], wa)
+    loads[0].wait()
+
+    def keys(r):
+        k1[r] = dg(ctx[r], matrix(wa), NN).astype(BF16)
+
+    blocks(T, 256, keys)
+    save(k1, k1_o)
+    eng.step(3)
+    fetch(1, [1], wb)
+
+    def values(r):
+        v1[r] = dg(ctx[r], matrix(wb), NN).astype(BF16)
+
+    blocks(T, 256, values)
+    save(v1, v1_o)
+    eng.step(4)
+    fetch(2, [2], packed)
+    norms[...] = norm_rows(packed[...].reshape((-1,) + packed.shape[3:]))
+    save(norms, norms_o)
+    loads[1].wait()
+
+    def first_norm(r):
+        normal, _ = moments(tok[r].astype(F32))
+        h1[r] = (normal * norms[0:1] + norms[1:2]).astype(BF16)
+
+    blocks(T, 128, first_norm)
+    save(h1, h1_o)
+    eng.step(5)
+    fetch(3, [3], wa)
+
+    def queries(r):
+        q1[r] = dg(h1[r], matrix(wa), NN).astype(BF16)
+
+    blocks(T, 256, queries)
+    save(q1, q1_o)
+
+    def heads(ticks, body):
+        def go(i, _):
+            def at(side):
+                for t, p in ticks:
+                    if p % 2 == side:
+                        pl.when(i == p // 2)(functools.partial(eng.step, t))
+
+            body(i, at)
+            return 0
+
+        lax.fori_loop(0, 6, go, 0)
+
+    heads(
+        ticks_cross,
+        lambda i, at: fwd_kernel(
+            frames, pair(q1, i), pair(k1, i), pair(v1, i), pair(o1, i), lse1.at[pl.ds(i, 1)], vt, ot,
+            causal=False, bq=512, unit=FRAME_TOK, at=at,
+        ),
+    )
+    save(o1, o1_o)
+    save(lse1, lse1_o)
+    fetch(4, [4], wb)
+    fetch(5, [5, 6, 7], wqkv)
+
+    def middle(r):
+        x = tok[r].astype(F32) + dg(o1[r], matrix(wb), NN)
+        x1[r] = x
+        normal, _ = moments(x)
+        h2[r] = (normal * norms[2:3] + norms[3:4]).astype(BF16)
+        for c in range(3):
+            qkv[r, c * D : (c + 1) * D] = dg(h2[r], matrix(wqkv, c * D), NN).astype(BF16)
+
+    blocks(T, 256, middle)
+    for ref, out in ((x1, x1_o), (h2, h2_o), (qkv, qkv_o)):
+        save(ref, out)
+    heads(
+        ticks_causal,
+        lambda i, at: fwd_kernel(
+            clip, pair(qkv, i), pair(qkv, i, D), pair(qkv, i, 2 * D), pair(o2, i), lse2.at[pl.ds(i, 1)], vt, ot,
+            causal=True, bq=512, unit=1, at=at,
+        ),
+    )
+    save(o2, o2_o)
+    save(lse2, lse2_o)
+    fetch(6, [8], wa)
+
+    def late(r):
+        x = x1[r] + dg(o2[r], matrix(wa), NN)
+        x2[r] = x
+        normal, _ = moments(x)
+        h3[r] = (normal * norms[4:5] + norms[5:6]).astype(BF16)
+
+    blocks(T, 256, late)
+    save(x2, x2_o)
+    save(h3, h3_o)
+    taken = [t for t, _ in ticks_cross + ticks_causal]
+    for t in range(6, eng.steps):
+        if t not in taken:
+            eng.step(t)
+    eng.arrive(range(9, len(eng.pieces)))
+    eng.sent()
+    for c in saves:
+        c.wait()
+
+
+def forward(clip, frames, tok, ctx, shards, n, cid):
+    eng = Gather([s.shape for s in shards], n)
+    T = tok.shape[0]
+    wide = jax.ShapeDtypeStruct((T, D), BF16)
+    full = jax.ShapeDtypeStruct((T, D), F32)
+    lse = jax.ShapeDtypeStruct((6, 2, T), F32)
+    kept = [wide] * 5 + [full, wide, jax.ShapeDtypeStruct((T, 3 * D), BF16), wide, full, wide, lse, lse]
+    kept.append(jax.ShapeDtypeStruct((16, D), F32))
+    own = shards[0].shape[0]
+    square = pltpu.VMEM(eng.dims + (own, D), BF16)
+    any_ = pl.BlockSpec(memory_space=pl.ANY)
+    smem = pl.BlockSpec(memory_space=pltpu.SMEM)
+    sem = pltpu.SemaphoreType.DMA
+    ticks_cross = [(6 + k, 2 * k + 1) for k in range(6)]
+    ticks_causal = [(12 + k, 3 * k) for k in range(4)]
+    outs = pl.pallas_call(
+        functools.partial(forward_kernel, eng, ticks_cross, ticks_causal),
+        out_shape=eng.outs() + kept,
+        in_specs=[smem, smem] + [any_] * (2 + eng.count),
+        out_specs=[any_] * (eng.count + len(kept)),
+        scratch_shapes=[pltpu.VMEM((T, D), BF16)] * 2
+        + [pltpu.VMEM(kept[i].shape, kept[i].dtype) for i in (0, 1, 2, 3, 4, 5, 6, 7, 8, 9, 10, 11, 12, 13)]
+        + [pltpu.VMEM(eng.dims + shards[2].shape, BF16), square, square]
+        + [pltpu.VMEM(eng.dims + (own, 3 * D), BF16), pltpu.VMEM((128, T), BF16), pltpu.VMEM((128, T), F32)]
+        + [sem((2,)), sem, sem((16,))]
+        + eng.scratch(),
+        compiler_params=pltpu.CompilerParams(
+            collective_id=cid, has_side_effects=True, vmem_limit_bytes=VMEM_BYTES
+        ),
+        name="forward",
+    )(clip, frames, tok, ctx, *shards)
+    return outs[: eng.count], outs[eng.count :]
 
 
 def shards(
@@ -638,36 +847,53 @@
         arrays = [g.reshape(grid_of(n) + g.shape[1:]) for g, _ in grads]
         return Scatter([a.shape[3:] for a in arrays], [t for _, t in grads], n), arrays
 
-    first, operands = gather([norms, cross_q, cross_k, cross_v])
-    norms, *whole = alone(first, operands, 0, "gather_cross")
-    w_q, w_k, w_v = flat(whole)
-    norms = norms.reshape((n,) + norms.shape[3:])[:, :6, :own].transpose(1, 0, 2).reshape(6, D).astype(F32)
-    gain_one, bias_one, gain_two, bias_two, gain_three, bias_three = [norms[i] for i in range(6)]
-
-    normal_one, inverse_one = moments(stream_in)
-    h1 = (normal_one * gain_one + bias_one).astype(BF16)
-    q1 = dg(h1, w_q, NN).astype(BF16)
-    k1 = dg(context_rows, w_k, NN).astype(BF16)
-    v1 = dg(context_rows, w_v, NN).astype(BF16)
-    second, operands = gather([cross_out, attn_qkv, attn_out])
-    (o1, lse1), whole = attn_fwd(
-        context_frames, q1, k1, v1, (0, 0, 0), False, FRAME_TOK, 512,
-        second, operands, paced(second, 8.0, 4.8, 2.2), 1, "cross_fwd",
-    )
-    w_o, w_qkv, w_p = flat(whole)
-    x1 = stream_in + dg(o1, w_o, NN)
-    normal_two, inverse_two = moments(x1)
-    h2 = (normal_two * gain_two + bias_two).astype(BF16)
-    qkv = dg(h2, w_qkv, NN).astype(BF16)
-    third, operands = gather([mlp_up, mlp_down])
-    (o2, lse2), whole = attn_fwd(
-        clip_lengths, qkv, qkv, qkv, (0, 6, 12), True, 1, 512,
-        third, operands, paced(third, 8.0, 4.8, 1.5), 2, "causal_fwd",
-    )
-    w_up, w_down = flat(whole)
-    x2 = x1 + dg(o2, w_p, NN)
-    normal_three, inverse_three = moments(x2)
-    h3 = (normal_three * gain_three + bias_three).astype(BF16)
+    if own % 16 == 0:
+        whole, kept = forward(
+            clip_lengths,
+            context_frames,
+            tokens[0],
+            context_rows,
+            [cross_k, cross_v, norms, cross_q, cross_out, attn_qkv, attn_out, mlp_up, mlp_down],
+            n,
+            0,
+        )
+        w_k, w_v, _, w_q, w_o, w_qkv, w_p, w_up, w_down = flat(whole)
+        q1, k1, v1, o1, h1, x1, h2, qkv, o2, x2, h3, lse1, lse2, norms = kept
+        gain_one, bias_one, gain_two, bias_two, gain_three, bias_three = [norms[i] for i in range(6)]
+        normal_one, inverse_one = moments(stream_in)
+        normal_two, inverse_two = moments(x1)
+        normal_three, inverse_three = moments(x2)
+    else:
+        first, operands = gather([norms, cross_q, cross_k, cross_v])
+        norms, *whole = alone(first, operands, 0, "gather_cross")
+        w_q, w_k, w_v = flat(whole)
+        norms = norms.reshape((n,) + norms.shape[3:])[:, :6, :own].transpose(1, 0, 2).reshape(6, D).astype(F32)
+        gain_one, bias_one, gain_two, bias_two, gain_three, bias_three = [norms[i] for i in range(6)]
+
+        normal_one, inverse_one = moments(stream_in)
+        h1 = (normal_one * gain_one + bias_one).astype(BF16)
+        q1 = dg(h1, w_q, NN).astype(BF16)
+        k1 = dg(context_rows, w_k, NN).astype(BF16)
+        v1 = dg(context_rows, w_v, NN).astype(BF16)
+        second, operands = gather([cross_out, attn_qkv, attn_out])
+        (o1, lse1), whole = attn_fwd(
+            context_frames, q1, k1, v1, (0, 0, 0), False, FRAME_TOK, 512,
+            second, operands, paced(second, 8.0, 4.8, 2.2), 1, "cross_fwd",
+        )
+        w_o, w_qkv, w_p = flat(whole)
+        x1 = stream_in + dg(o1, w_o, NN)
+        normal_two, inverse_two = moments(x1)
+        h2 = (normal_two * gain_two + bias_two).astype(BF16)
+        qkv = dg(h2, w_qkv, NN).astype(BF16)
+        third, operands = gather([mlp_up, mlp_down])
+        (o2, lse2), whole = attn_fwd(
+            clip_lengths, qkv, qkv, qkv, (0, 6, 12), True, 1, 512,
+            third, operands, paced(third, 8.0, 4.8, 1.5), 2, "causal_fwd",
+        )
+        w_up, w_down = flat(whole)
+        x2 = x1 + dg(o2, w_p, NN)
+        normal_three, inverse_three = moments(x2)
+        h3 = (normal_three * gain_three + bias_three).astype(BF16)
     up = dg(h3, w_up, NN)
     hidden = gelu(up).astype(BF16)
     x3 = x2 + dg(hidden, w_down, NN)

time: 493 us -> 428 us (0.87); the launches traced: 484 us -> 424 us
  local copies, waits for them, and re-layouts: 29.1 us -> 7.26 us
  other arithmetic: 27.4 us -> 12.8 us
  matrix products: 119 us -> 105 us
  Pallas kernels: 306 us -> 296 us
    pallas_call x0 -> x1, Pallas kernels: none -> 134 us  [forward(): pl.pallas_call(functools.partial(forward_kernel, eng, ticks_cross, ticks_...]
    pallas_call x4 -> x2, Pallas kernels: 237 us -> 128 us  [attend_beside(): pl.pallas_call(kernel, grid=(6,), in_specs=in_specs + [any_] * moved, out...]
    pallas_call x2 -> x1, Pallas kernels: 65.1 us -> 31.3 us  [alone(): pl.pallas_call(kernel, out_shape=engine.outs(), in_specs=[pl.BlockSpec(me...]
    unnamed x82 -> x58, local copies, waits for them, and re-layouts: 18.5 us -> 3.82 us
    dot_general x26 -> x20, matrix products: 119 us -> 105 us  [dg(): return lax.dot_general(a, b, dims, preferred_element_type=F32)]
    dot_general x2 -> x0, local copies, waits for them, and re-layouts: 7.48 us -> none  [dg(): return lax.dot_general(a, b, dims, preferred_element_type=F32)]
    reduce_sum x2 -> x0, other arithmetic: 6.77 us -> none  [norm_back(): return (back, jnp.sum(grad * normal, 0), jnp.sum(grad, 0))]
    add x1, other arithmetic: 6.43 us -> 1.24 us  [shards(): dx1 = dx2 + back]
where the time goes in v4:
time: 428 us; the launch traced here: 424 us
  Pallas kernels  296 us (69%)
  matrix products  105 us (25%)
  other arithmetic  12.8 us (3%)
  local copies, waits for them, and re-layouts  7.26 us (2%)
    pallas_call x1, Pallas kernels, forward(): pl.pallas_call(functools.partial(forward_kernel, eng, ticks_cross, ticks_...  134 us
    pallas_call x2, Pallas kernels, attend_beside(): pl.pallas_call(kernel, grid=(6,), in_specs=in_specs + [any_] * moved, out...  128 us
    dot_general x20, matrix products, dg(): return lax.dot_general(a, b, dims, preferred_element_type=F32)  105 us
    pallas_call x1, Pallas kernels, alone(): pl.pallas_call(kernel, out_shape=engine.outs(), in_specs=[pl.BlockSpec(me...  31.3 us

profile of v4, /device:TPU:0, one launch (start us, length us, event | category | flops | bytes accessed | tf_op | source)
XLA Modules:
  0.0 424.4 jit_solution(15699838559658333076)
XLA Ops:
  3.3 133.8 %forward.1 = (bf16[4,2,2,48,768]{4,3,2,1,0:T(8,128)(2,1)}, bf16[4,2,2,48,768]{4,3,2,1,0:T(8,128)(2,1)}, bf16[4,2,2,16,256]{4,3,2,1,0:T(8,128)(2,1)}, bf16[4,2,2,...) custom-call(s32[1]{0:T(128)} %copy.42.refs_0_, ...), custom_call_target="tpu_custom_call" | custom-call | tf_op jit(solution)/shard_map/forward/pallas_call | solution.py:787
  137.2 7.5 %fusion.90 = f32[1024,3072]{1,0:T(8,128)S(1)} fusion(bf16[1024,768]{1,0:T(8,128)(2,1)} %get-tuple-element.56, bf16[768,3072]{1,0:T(8,128)(2,1)} %bitcast.151), kind=kOutput, calls=%fused_computation.131 | convolution fusion | flops 4831838208 | bytes 18874368 | tf_op jit(solution)/shard_map/dot_general | solution.py:20
  144.7 8.8 %fusion.70 = bf16[1,1024,768]{2,1,0:T(8,128)(2,1)} fusion(f32[1024,768]{1,0:T(8,128)S(1)} %copy-done.1, bf16[3072,768]{1,0:T(8,128)(2,1)S(1)} %bitcast.153, pred[1024]{0:T(1024)(128)(4,1)S(1)} %iota_compare_fusion, f32[1024,3072]{1,0:T(8,128)S(1)} %fusion.90), kind=kOutput, calls=%fused_computation.83 | convolution fusion | flops 4862509056 | bytes 22021120 | tf_op jit(solution)/shard_map/dot_general | solution.py:20
  155.9 2.8 multiply_reduce_fusion.3
  159.7 13.5 %fusion.7 = bf16[1024,3072]{1,0:T(8,128)(2,1)} fusion(f32[1024,3072]{1,0:T(8,128)} %copy-done.23, bf16[3072,768]{1,0:T(8,128)(2,1)S(1)} %bitcast.154, bf16[1,1024,768]{2,1,0:T(8,128)(2,1)S(1)} %copy-done.10, pred[1024]{0:T(1024)(128)(4,1)S(1)} %iota_compare_fusion), kind=kOutput, calls=%fused_computation.9 | convolution fusion | flops 4893966336 | bytes 25166848 | tf_op jit(solution)/shard_map/dot_general | solution.py:20
  173.1 9.4 %multiply_reduce_fusion = (bf16[768]{0:T(1024)(128)(2,1)S(1)}, f32[1024]{0:T(1024)S(1)}, f32[1024]{0:T(1024)S(1)}, bf16[768]{0:T(1024)(128)(2,1)S(1)}, f32[1024,768]{1,0:T(8,128)S(1)}) fusion(f32[1024,768]{1,0:T(8,128)S(1)} %copy-done.2, f32[1024]{0:T(1024)S(1)} %add_rsqrt_fusion.2, f32[1024]{0:T(1024)S(1)} %broadcast_multiply_fusion.8, ...), kind=kOutput, calls=%fused_computation.33 | convolution fusion | flops 4838912000 | bytes 17324032 | tf_op jit(solution)/shard_map/dot_general | solution.py:20
  184.1 2.7 convolution_convert_fusion.3.refs_5_
  186.8 22.9 %convolution_convert_fusion.1 = bf16[3072,768]{1,0:T(8,128)(2,1)} fusion(bf16[1,1024,768]{2,1,0:T(8,128)(2,1)S(1)} %copy-done.10, pred[1024]{0:T(1024)(128)(4,1)S(1)} %iota_compare_fusion, f32[1024,3072]{1,0:T(8,128)} %copy-done.23), kind=kOutput, calls=%fused_computation.12 | convolution fusion | flops 4864868352 | bytes 18875392 | tf_op jit(solution)/shard_map/dot_general | solution.py:20
  209.7 6.8 %convolution_convert_fusion = bf16[768,3072]{1,0:T(8,128)(2,1)} fusion(bf16[1024,768]{1,0:T(8,128)(2,1)S(1)} %copy-done.19, bf16[1024,3072]{1,0:T(8,128)(2,1)S(1)} %bitcast.159), kind=kOutput, calls=%fused_computation.11 | convolution fusion | flops 4834197504 | bytes 12582912 | tf_op jit(solution)/shard_map/dot_general | solution.py:20
  216.5 69.7 %causal_bwd.1 = (bf16[3,1024,768]{2,1,0:T(8,128)(2,1)}, f32[48,3072]{1,0:T(8,128)}, f32[192,768]{1,0:T(8,128)}) custom-call(s32[1]{0:T(128)} %copy.42.refs_0_, bf16[1024,2304]{1,0:T(8,128)(2,1)} %get-tuple-element.61.refs_1_.refs_2_.refs_3_, bf16[1024,2304]{1,0:T(8,128)(2,1)} %get-tuple-element.61.refs_1_.refs_2_.refs_3_, ...), custom_call_target="tpu_custom_call" | custom-call | tf_op jit(solution)/shard_map/causal_bwd/pallas_call | solution.py:500
  286.3 3.3 fusion.44
  291.9 2.6 multiply_reduce_fusion.1
  298.2 2.6 convolution_convert_fusion.2.refs_5_
  300.7 2.5 convolution_convert_fusion.5
  308.2 2.5 fusion.58
  310.8 2.5 convolution_convert_fusion.4
  313.3 58.5 %cross_bwd.1 = (bf16[3,1024,768]{2,1,0:T(8,128)(2,1)}, f32[48,768]{1,0:T(8,128)}, f32[48,2304]{1,0:T(8,128)}, f32[48,768]{1,0:T(8,128)}) custom-call(s32[1]{0:T(128)S(6)} %copy.43.refs_1_.refs_0_, bf16[1024,768]{1,0:T(8,128)(2,1)} %get-tuple-element.67.refs_1_, bf16[1024,768]{1,0:T(8,128)(2,1)} %get-tuple-element.68.refs_2_, ...), custom_call_target="tpu_custom_call" | custom-call | tf_op jit(solution)/shard_map/cross_bwd/pallas_call | solution.py:500
  371.8 3.7 fusion.18
  375.5 2.6 fusion.17
  379.5 2.5 fusion.64
  382.0 2.5 fusion.67
  384.5 2.5 fusion.61
  388.3 31.3 %scatter_cross.1 = (f32[16,256]{1,0:T(8,128)}, f32[48,768]{1,0:T(8,128)}, f32[48,768]{1,0:T(8,128)}, f32[48,768]{1,0:T(8,128)}) custom-call(bf16[4,2,2,48,768]{4,3,2,1,0:T(8,128)(2,1)} %bitcast.132, bf16[4,2,2,48,768]{4,3,2,1,0:T(8,128)(2,1)} %bitcast.133, bf16[4,2,2,48,768]{4,3,2,1,0:T(8,128)(2,1)} %bitcast.134, bf16[4,2,2,16,256]{4,3,2,1,0:T(8,128)(2,1)} %bitcast.140), custom_call_target="tpu_custom_call" | custom-call | tf_op jit(solution)/shard_map/scatter_cross/pallas_call | solution.py:429
  421.0 3.3 finish.1
  (93 shorter events, 21.1 us)
Async XLA Ops:
  137.1 7.5 %copy-start.1 = (f32[1024,768]{1,0:T(8,128)S(1)}, f32[1024,768]{1,0:T(8,128)}, u32[]{:S(2)}) copy-start(f32[1024,768]{1,0:T(8,128)} %get-tuple-element.55) | copy-start | bytes 9437188
  137.1 7.5 %copy-start.14 = (bf16[4,2,2,192,768]{4,3,2,1,0:T(8,128)(2,1)S(1)}, bf16[4,2,2,192,768]{4,3,2,1,0:T(8,128)(2,1)}, u32[]{:S(2)}) copy-start(bf16[4,2,2,192,768]{4,3,2,1,0:T(8,128)(2,1)} %get-tuple-element.58) | copy-start | bytes 14155780
  144.7 8.8 %copy-start.23 = (f32[1024,3072]{1,0:T(8,128)}, f32[1024,3072]{1,0:T(8,128)S(1)}, u32[]{:S(2)}) copy-start(f32[1024,3072]{1,0:T(8,128)S(1)} %fusion.90) | copy-start | bytes 37748740
  144.7 8.8 %copy-start = (f32[1024,768]{1,0:T(8,128)S(1)}, f32[1024,768]{1,0:T(8,128)}, u32[]{:S(2)}) copy-start(f32[1024,768]{1,0:T(8,128)} %get-tuple-element.60) | copy-start | bytes 9437188
  155.9 3.8 copy-start.10
  155.9 3.8 copy-start.15
  159.6 13.5 %copy-start.2 = (f32[1024,768]{1,0:T(8,128)S(1)}, f32[1024,768]{1,0:T(8,128)}, u32[]{:S(2)}) copy-start(f32[1024,768]{1,0:T(8,128)} %get-tuple-element.55) | copy-start | bytes 9437188
  184.1 2.8 copy-start.4
  184.1 25.6 %slice-start = ((s8[6291456]{0:T(1024)(128)(4,1)}), s8[4194304]{0:T(1024)(128)(4,1)S(1)}, s32[]{:S(2)}) async-start(s8[6291456]{0:T(1024)(128)(4,1)} %bitcast.158), calls=%async_computation | async-start | bytes 8388608
  186.8 22.9 %copy-start.19 = (bf16[1024,768]{1,0:T(8,128)(2,1)S(1)}, bf16[1024,768]{1,0:T(8,128)(2,1)}, u32[]{:S(2)}) copy-start(bf16[1024,768]{1,0:T(8,128)(2,1)} %get-tuple-element.56) | copy-start | bytes 4718596
  186.8 22.9 %slice-start.1 = ((s8[6291456]{0:T(1024)(128)(4,1)}), s8[2097152]{0:T(1024)(128)(4,1)S(1)}, s32[]{:S(2)}) async-start(s8[6291456]{0:T(1024)(128)(4,1)} %bitcast.158), calls=%async_computation.1 | async-start | bytes 4194304
  286.2 3.3 copy-start.12
  286.2 4.3 %copy-start.13 = (bf16[4,2,2,48,2304]{4,3,2,1,0:T(8,128)(2,1)S(1)}, bf16[4,2,2,48,2304]{4,3,2,1,0:T(8,128)(2,1)}, u32[]{:S(2)}) copy-start(bf16[4,2,2,48,2304]{4,3,2,1,0:T(8,128)(2,1)} %get-tuple-element.66) | copy-start | bytes 10616836
  291.9 2.7 copy-start.5
  296.0 14.7 %copy-start.6 = (f32[1024,768]{1,0:T(8,128)}, f32[1024,768]{1,0:T(8,128)S(1)}, u32[]{:S(2)}) copy-start(f32[1024,768]{1,0:T(8,128)S(1)} %multiply_add_fusion.1) | copy-start | bytes 9437188
  296.0 2.1 copy-start.21
  298.1 2.6 copy-start.8
  300.7 2.5 copy-start.18
  308.2 2.5 copy-start.11
  313.3 58.5 %copy-start.20 = (bf16[4,2,2,48,768]{4,3,2,1,0:T(8,128)(2,1)S(1)}, bf16[4,2,2,48,768]{4,3,2,1,0:T(8,128)(2,1)}, u32[]{:S(2)}) copy-start(bf16[4,2,2,48,768]{4,3,2,1,0:T(8,128)(2,1)} %get-tuple-element.75) | copy-start | bytes 3538948
  371.8 3.8 copy-start.7
  375.5 2.6 copy-start.9
  375.5 3.9 copy-start.16
  382.0 2.5 copy-start.17
  (2 other events, 3.0 us)
